TPU v7x, 32 devices: a whole 2x2x4 slice. The times are simulated.
32 devices in a mesh: seq: 16 (over z, y, x), head: 2 (over core).
Axes of the slice: x: 2, y: 2, z: 4, core: 2. Of those that a mesh axis runs over, the one named last changes fastest.
Arguments:
- tokens: bfloat16 [8192, 1536], P('seq', 'head'), may hold values from -6 to 6
- cotangent: bfloat16 [8192, 1536], P('seq', 'head'), may hold values from -6 to 6
- seg_ids: int32 [8192], P('seq'), may hold values from 0 to 8191, as said below
- carry_flags: int32 [32], P('seq'), may hold values from 0 to 1, as said below
- inner_weight: float32 [1536, 2, 3072], P('seq', None, 'head'), may hold values from -0.15625 to 0.15625
- inner_velocity: float32 [1536, 2, 3072], P('seq', None, 'head'), may hold values from -192 to 192
- inner_average: float32 [1536, 2, 3072], P('seq', None, 'head'), may hold values from -0.15625 to 0.15625
- groups_weight: float32 [1536, 256], P('seq', 'head'), may hold values from -0.15625 to 0.15625
- groups_velocity: float32 [1536, 256], P('seq', 'head'), may hold values from -192 to 192
- groups_average: float32 [1536, 256], P('seq', 'head'), may hold values from -0.15625 to 0.15625
- stepper_weight: float32 [1536, 48], P('seq', 'head'), may hold values from -0.078125 to 0.078125
- stepper_velocity: float32 [1536, 48], P('seq', 'head'), may hold values from -192 to 192
- stepper_average: float32 [1536, 48], P('seq', 'head'), may hold values from -0.078125 to 0.078125
- outer_weight: float32 [3072, 1536], P('head', 'seq'), may hold values from -0.109375 to 0.109375
- outer_velocity: float32 [3072, 1536], P('head', 'seq'), may hold values from -192 to 192
- outer_average: float32 [3072, 1536], P('head', 'seq'), may hold values from -0.109375 to 0.109375
- filters_weight: float32 [5, 3072], P(None, 'head'), may hold values from -3 to 3
- filters_velocity: float32 [5, 3072], P(None, 'head'), may hold values from -192 to 192
- filters_average: float32 [5, 3072], P(None, 'head'), may hold values from -3 to 3
- probes_weight: float32 [5, 256], P(None, 'head'), may hold values from -3 to 3
- probes_velocity: float32 [5, 256], P(None, 'head'), may hold values from -192 to 192
- probes_average: float32 [5, 256], P(None, 'head'), may hold values from -3 to 3
- prenorm_weight: float32 [1536], replicated, may hold values from 0.5 to 1.5
- prenorm_velocity: float32 [1536], replicated, may hold values from -192 to 192
- prenorm_average: float32 [1536], replicated, may hold values from -1 to 1
- postnorm_weight: float32 [3072], P('head'), may hold values from 0.5 to 1.5
- postnorm_velocity: float32 [3072], P('head'), may hold values from -192 to 192
- postnorm_average: float32 [3072], P('head'), may hold values from -1 to 1
- heads_weight: float32 [3, 48], P(None, 'head')
- heads_velocity: float32 [3, 48], P(None, 'head'), may hold values from -192 to 192
- heads_average: float32 [3, 48], P(None, 'head'), may hold values from -1 to 1
Outputs:
- output: bfloat16 [8192, 1536], P('seq', 'head')
- input_gradient: float32 [8192, 1536], P('seq', 'head')
- inner_gradient: float32 [1536, 2, 3072], P('seq', None, 'head')
- inner_master: float32 [1536, 2, 3072], P('seq', None, 'head')
- inner_momentum: float32 [1536, 2, 3072], P('seq', None, 'head')
- inner_smoothed: float32 [1536, 2, 3072], P('seq', None, 'head')
- groups_gradient: float32 [1536, 256], P('seq', 'head')
- groups_master: float32 [1536, 256], P('seq', 'head')
- groups_momentum: float32 [1536, 256], P('seq', 'head')
- groups_smoothed: float32 [1536, 256], P('seq', 'head')
- stepper_gradient: float32 [1536, 48], P('seq', 'head')
- stepper_master: float32 [1536, 48], P('seq', 'head')
- stepper_momentum: float32 [1536, 48], P('seq', 'head')
- stepper_smoothed: float32 [1536, 48], P('seq', 'head')
- outer_gradient: float32 [3072, 1536], P('head', 'seq')
- outer_master: float32 [3072, 1536], P('head', 'seq')
- outer_momentum: float32 [3072, 1536], P('head', 'seq')
- outer_smoothed: float32 [3072, 1536], P('head', 'seq')
- filters_gradient: float32 [5, 3072], P(None, 'head')
- filters_master: float32 [5, 3072], P(None, 'head')
- filters_momentum: float32 [5, 3072], P(None, 'head')
- filters_smoothed: float32 [5, 3072], P(None, 'head')
- probes_gradient: float32 [5, 256], P(None, 'head')
- probes_master: float32 [5, 256], P(None, 'head')
- probes_momentum: float32 [5, 256], P(None, 'head')
- probes_smoothed: float32 [5, 256], P(None, 'head')
- prenorm_gradient: float32 [1536], replicated
- prenorm_master: float32 [1536], replicated
- prenorm_momentum: float32 [1536], replicated
- prenorm_smoothed: float32 [1536], replicated
- postnorm_gradient: float32 [3072], P('head')
- postnorm_master: float32 [3072], P('head')
- postnorm_momentum: float32 [3072], P('head')
- postnorm_smoothed: float32 [3072], P('head')
- heads_gradient: float32 [3, 48], P(None, 'head')
- heads_master: float32 [3, 48], P(None, 'head')
- heads_momentum: float32 [3, 48], P(None, 'head')
- heads_smoothed: float32 [3, 48], P(None, 'head')
Inputs may be any that keep to these rules, and one draw needn't show every extreme that they name: seg_ids[t] is the position of the first token of t's document, so it never falls; a new document begins at every multiple of 8192 and at the last token. carry_flags[c] is 0 where a document begins at token c * 256, else 1.
All inputs are finite; a program needn't handle non-finite values.
Results may differ from a plain program's by a relative error of at most 0.0038.
The roundings to bfloat16 on the way count: a program that leaves them out, or rounds other values in their place, can miss the bound.
Values may be sent and summed in bfloat16 or wider, within the bound.
No kernel may reach another device: no remote copies, remote signals or barrier semaphores. Data moves between devices by JAX's collectives and lax.ppermute only.
A program may use at most 256 MiB of HBM per device.

v0:
```python
import math

import jax
import jax.numpy as jnp
from jax import lax
from jax.experimental import pallas as pl
from jax.experimental.pallas import tpu as pltpu
from jax.sharding import PartitionSpec as P


D = 1536
DI = 3072
P_SIZE = 64
N = 128
KC = 4
CH = 256
HB = 8
SEQ = "seq"
HEAD = "head"


epsilon = 1e-05
momentum_decay = 0.9
average_decay = 0.9
highest = lax.Precision.HIGHEST
f32 = jnp.float32
bf16 = jnp.bfloat16


def shifted(array, axis, by):
    count = lax.axis_size(axis)
    pairs = [(i, i + by) for i in range(count) if 0 <= i + by < count]
    return lax.ppermute(array, axis, pairs)


def swap(array, axis, mask):
    count = lax.axis_size(axis)
    return lax.ppermute(array, axis, [(i, i ^ mask) for i in range(count)])


def bit_orders(axis):
    bits = lax.axis_size(axis).bit_length() - 1
    first = list(range(bits))
    second = first[:]
    if bits > 1:
        second[0], second[1] = 1, 0
    return first, second


def after(values, *others):
    return lax.optimization_barrier((values, others))[0]


def assemble(own, other, axis, bit, done):
    upper = ((lax.axis_index(axis) >> bit) & 1) == 1
    before = 1 << sum(1 for b in done if b > bit)
    split = (before, own.shape[0] // before, own.shape[1])
    own, other = own.reshape(split), other.reshape(split)
    return jnp.stack([jnp.where(upper, other, own), jnp.where(upper, own, other)], 1).reshape(
        2 * split[0] * split[1], split[2]
    )


def gather_rows(held, axis, bits, done=()):
    done = list(done)
    for bit in bits:
        held = assemble(held, swap(held, axis, 1 << bit), axis, bit, done)
        done.append(bit)
    return held


def sides_of(held, axis, bit, left):
    mine = (lax.axis_index(axis) >> bit) & 1
    before = 1 << sum(1 for b in left if b > bit)
    split = held.reshape(before, 2, held.shape[0] // (2 * before), held.shape[1])
    flat = (held.shape[0] // 2, held.shape[1])
    kept = lax.dynamic_index_in_dim(split, mine, 1, False).reshape(flat)
    return kept, lax.dynamic_index_in_dim(split, 1 - mine, 1, False).astype(bf16).reshape(flat)


def scatter_rows(held, axis, bits, left):
    left = list(left)
    for bit in bits:
        kept, sent = sides_of(held, axis, bit, left)
        held = kept + swap(sent, axis, 1 << bit).astype(f32)
        left.remove(bit)
    return held


def pick_columns(array, axis, bit, other):
    mine = (lax.axis_index(axis) >> bit) & 1
    run = (array.shape[1] // lax.axis_size(axis)) << bit
    split = array.reshape(array.shape[0], array.shape[1] // (2 * run), 2, run)
    return lax.dynamic_index_in_dim(split, 1 - mine if other else mine, 2, False).reshape(
        array.shape[0], array.shape[1] // 2
    )


def token_product(left, right):
    return lax.dot_general(left, right, (((0,), (0,)), ((), ())), preferred_element_type=f32)


def butterfly_sum(array, axis, bits):
    for bit in bits:
        array = array + swap(array, axis, 1 << bit)
    return array


def side_by_side(own, other, upper):
    return jnp.concatenate([jnp.where(upper, other, own), jnp.where(upper, own, other)], 1)


def expand(array):
    count = array.shape[-1]
    spread = (
        jnp.arange(count)[:, None] == (jnp.arange(count * P_SIZE) // P_SIZE)[None, :]
    ).astype(f32)
    return jnp.dot(array, spread, precision=highest)


def silu_slope(values):
    sigmoid = jax.nn.sigmoid(values)
    return sigmoid * (1.0 + values * (1.0 - sigmoid))


def tap_masks(seg_rows, flag_rows, span_len, taps):
    number = seg_rows.shape[0]
    within = jnp.arange(number) % span_len
    first_seg = jnp.repeat(seg_rows[::span_len], span_len)
    continued = (jnp.repeat(flag_rows, span_len) == 1) & (seg_rows == first_seg)
    stacked = []
    for lagged in range(1, taps):
        earlier = jnp.concatenate([jnp.full((lagged,), -1, jnp.int32), seg_rows[:-lagged]])
        stacked.append(jnp.where(within >= lagged, earlier == seg_rows, continued))
    return jnp.stack(stacked).astype(jnp.float32)


def conv_apply(extended, tap_rows, masks, taps):
    number = extended.shape[0] - (taps - 1)
    total = tap_rows[taps] + tap_rows[0] * extended[taps - 1 :]
    for lagged in range(1, taps):
        begin = taps - 1 - lagged
        total = (
            total + tap_rows[lagged] * masks[lagged - 1][:, None] * extended[begin : begin + number]
        )
    return total


def conv_backward(extended, tap_rows, masks, grads, taps):
    number = grads.shape[0]
    tap_grads = [jnp.sum(grads * extended[taps - 1 :], 0)]
    ext_grad = jnp.pad(tap_rows[0] * grads, ((taps - 1, 0), (0, 0)))
    for lagged in range(1, taps):
        masked = masks[lagged - 1][:, None] * grads
        begin = taps - 1 - lagged
        tap_grads.append(jnp.sum(masked * extended[begin : begin + number], 0))
        ext_grad = ext_grad + jnp.pad(tap_rows[lagged] * masked, ((begin, lagged), (0, 0)))
    tap_grads.append(jnp.sum(grads, 0))
    return (jnp.stack(tap_grads), ext_grad)


def span_edges(log_decay, seg_spans, flag_spans):
    length = log_decay.shape[1]
    lower = (jnp.arange(length)[:, None] >= jnp.arange(length)[None, :]).astype(f32)
    cumulative = jnp.einsum("ij,cjh->cih", lower, log_decay, precision=highest)
    carried = flag_spans.astype(jnp.float32)[:, None] * (seg_spans == seg_spans[:, :1]).astype(
        jnp.float32
    )
    keeping = (seg_spans == seg_spans[:, -1:]).astype(jnp.float32)
    entering = carried[:, :, None] * jnp.exp(cumulative)
    leaving = keeping[:, :, None] * jnp.exp(cumulative[:, -1:, :] - cumulative)
    chained = carried[:, -1:] * jnp.exp(cumulative[:, -1, :])
    return (cumulative, entering, leaving, chained)


def apply_update(master, velocity, average, gradient, rate_value):
    moment = momentum_decay * velocity + gradient
    stepped = master - rate_value * (gradient + momentum_decay * moment)
    smoothed = average_decay * average + (1.0 - average_decay) * stepped
    return (gradient, stepped, moment, smoothed)


def walk_kernel(count, reverse, part_ref, factor_ref, out_ref):
    def one(turn, state):
        source = count - 1 - turn if reverse else turn
        out_ref[source] = state
        return factor_ref[source] * state + part_ref[source, :, : state.shape[1]]

    lax.fori_loop(0, count, one, jnp.zeros(out_ref.shape[1:], f32))


def parts_out(part, axis):
    count = lax.axis_size(axis)
    pieces = part.reshape((count, part.shape[0] // count) + part.shape[1:])
    return lax.all_to_all(pieces, axis, 0, 0)


def walked_in(pieces, factors, axis, reverse):
    count = lax.axis_size(axis)
    rows, width = pieces.shape[1], factors.shape[2]
    walked = pl.pallas_call(
        lambda *refs: walk_kernel(count, reverse, *refs),
        out_shape=jax.ShapeDtypeStruct((count, rows, width), f32),
        name="walk",
    )(pieces, factors)
    back = lax.all_to_all(walked, axis, 0, 0)
    return walked, back.reshape(count * rows, width)


def update_kernel(rate_value, gate_ref, rest_ref, w_ref, v_ref, a_ref, g_out, w_out, v_out, a_out):
    for k, grad_ref in ((0, gate_ref), (1, rest_ref)):
        grad = grad_ref[...]
        moment = momentum_decay * v_ref[:, k, :] + grad
        stepped = w_ref[:, k, :] - rate_value * (grad + momentum_decay * moment)
        g_out[:, k, :] = grad
        w_out[:, k, :] = stepped
        v_out[:, k, :] = moment
        a_out[:, k, :] = average_decay * a_ref[:, k, :] + (1.0 - average_decay) * stepped


def update_inner(weight, velocity, average, gate_grad, rest_grad, rate_value):
    rows, two, width = weight.shape
    step = 32 if rows % 32 == 0 else rows
    flat = pl.BlockSpec((step, width), lambda r: (r, 0))
    deep = pl.BlockSpec((step, two, width), lambda r: (r, 0, 0))
    return pl.pallas_call(
        lambda *refs: update_kernel(rate_value, *refs),
        grid=(rows // step,),
        in_specs=[flat, flat, deep, deep, deep],
        out_specs=[deep] * 4,
        out_shape=[jax.ShapeDtypeStruct(weight.shape, f32)] * 4,
        name="update_inner",
    )(gate_grad, rest_grad, weight, velocity, average)


def masked_bias(seg_row, seg_col):
    length = seg_row.shape[1]
    rows = lax.broadcasted_iota(jnp.int32, (length, length), 0)
    cols = lax.broadcasted_iota(jnp.int32, (length, length), 1)
    return jnp.where((rows >= cols) & (seg_col == seg_row), 0.0, -1e30).astype(f32)


def inner_product(one, two):
    return lax.dot_general(one, two, (((1,), (1,)), ((), ())), preferred_element_type=f32)


def halves_of(array):
    high = array.astype(bf16)
    return high, (array - high.astype(f32)).astype(bf16)


def exact_dot(left, right, contract=((1,), (0,))):
    return sum(
        lax.dot_general(left, part, (contract, ((), ())), preferred_element_type=f32)
        for part in halves_of(right)
    )


def pair_columns(columns, pair, low_lanes):
    return jnp.where(
        low_lanes, columns[:, 2 * pair : 2 * pair + 1], columns[:, 2 * pair + 1 : 2 * pair + 2]
    )


def entry_state(first_ref, added_ref, chain_ref, lanes):
    first = first_ref[:, lanes]
    return jnp.where(
        pl.program_id(0) == 0, first, chain_ref[:, lanes] * first + added_ref[:, lanes]
    )


def gated_pieces(refs, pair, low_lanes, enter):
    local_ref, gate_ref, mixed_ref, c_ref, first_ref, added_ref, chain_ref, gain_ref = refs
    lanes = pl.ds(pair * 2 * P_SIZE, 2 * P_SIZE)
    enter_pair = pair_columns(enter, pair, low_lanes)
    states = entry_state(first_ref, added_ref, chain_ref, lanes)
    out = local_ref[:, lanes] + enter_pair * exact_dot(c_ref[...], states)
    gate = gate_ref[:, lanes]
    sigmoid = 1.0 / (1.0 + jnp.exp(-gate))
    act = gate * sigmoid
    return out, gate, sigmoid, act, out * act, mixed_ref[:, lanes], gain_ref[:, lanes], enter_pair


def row_sums_kernel(*refs):
    refs, (enter_ref, out_ref) = refs[:8], refs[8:]
    enter = enter_ref[...]
    lane = lax.broadcasted_iota(jnp.int32, (CH, 2 * P_SIZE), 1)
    squares = jnp.zeros((CH, 2 * P_SIZE), f32)
    dots = jnp.zeros((CH, 2 * P_SIZE), f32)
    for pair in range(refs[0].shape[1] // (2 * P_SIZE)):
        gated, d_mixed, gain = gated_pieces(refs, pair, lane < P_SIZE, enter)[4:7]
        squares = squares + gated * gated
        dots = dots + d_mixed * gain * gated
    out_ref[...] = jnp.where(
        lane == 0,
        jnp.sum(squares, 1, keepdims=True),
        jnp.where(lane == 1, jnp.sum(dots, 1, keepdims=True), 0.0),
    )


def middle_specs(width, heads):
    wide = pl.BlockSpec((CH, width), lambda s: (s, 0))
    state = pl.BlockSpec((N, width), lambda s: (0, 0))
    row = pl.BlockSpec((1, width), lambda s: (0, 0))
    group = pl.BlockSpec((CH, N), lambda s: (s, 0))
    return [wide, wide, wide, group, state, state, row, row, pl.BlockSpec((CH, heads), lambda s: (s, 0))]


def row_sums(*args):
    rows, width = args[0].shape
    return pl.pallas_call(
        row_sums_kernel,
        grid=(rows // CH,),
        in_specs=middle_specs(width, args[-1].shape[1]),
        out_specs=pl.BlockSpec((CH, 2 * P_SIZE), lambda s: (s, 0)),
        out_shape=jax.ShapeDtypeStruct((rows, 2 * P_SIZE), f32),
        name="row_sums",
    )(*args)


def middle_kernel(*all_refs):
    refs, (enter_ref, own_ref, other_ref) = all_refs[:8], all_refs[8:11]
    mixed_out, ssd_out, gate_out, post_out, total_out, last_out = all_refs[11:]
    c_ref, chain_ref = refs[3], refs[6]

    @pl.when(pl.program_id(0) == 0)
    def _():
        post_out[...] = jnp.zeros_like(post_out)
        total_out[...] = jnp.zeros_like(total_out)

    enter = enter_ref[...]
    both = own_ref[...] + other_ref[...]
    scale = lax.rsqrt(both[:, 0:1] / DI + epsilon)
    pulled = scale * scale * scale * (both[:, 1:2] / DI)
    low_lanes = lax.broadcasted_iota(jnp.int32, (CH, 2 * P_SIZE), 1) < P_SIZE
    for pair in range(refs[0].shape[1] // (2 * P_SIZE)):
        lanes = pl.ds(pair * 2 * P_SIZE, 2 * P_SIZE)
        out, gate, sigmoid, act, gated, d_mixed, gain, enter_pair = gated_pieces(
            refs, pair, low_lanes, enter
        )
        mixed_out[:, lanes] = (gated * scale * gain).astype(bf16)
        d_gated = scale * (d_mixed * gain) - gated * pulled
        d_ssd = (d_gated * act).astype(bf16)
        ssd_out[:, lanes] = d_ssd
        gate_out[:, lanes] = (d_gated * out * (sigmoid * (1.0 + gate * (1.0 - sigmoid)))).astype(bf16)
        post_out[:, lanes] += jnp.sum(d_mixed * gated * scale, 0, keepdims=True)
        pull = exact_dot(c_ref[...], enter_pair * d_ssd.astype(f32), ((0,), (0,)))
        total_out[:, lanes] += jnp.where(pl.program_id(0) == 0, 1.0, chain_ref[:, lanes]) * pull
        last_out[:, lanes] = pull


def middle(*args):
    rows, width = args[0].shape
    wide = pl.BlockSpec((CH, width), lambda s: (s, 0))
    state = pl.BlockSpec((N, width), lambda s: (0, 0))
    low = jax.ShapeDtypeStruct((rows, width), bf16)
    return pl.pallas_call(
        middle_kernel,
        grid=(rows // CH,),
        in_specs=middle_specs(width, args[-3].shape[1])
        + [pl.BlockSpec((CH, 2 * P_SIZE), lambda s: (s, 0))] * 2,
        out_specs=[wide, wide, wide, pl.BlockSpec((1, width), lambda s: (0, 0)), state, state],
        out_shape=[
            low,
            low,
            low,
            jax.ShapeDtypeStruct((1, width), f32),
            jax.ShapeDtypeStruct((N, width), f32),
            jax.ShapeDtypeStruct((N, width), f32),
        ],
        name="middle",
    )(*args)


def late_kernel(v_ref, g_ref, b_ref, c_ref, first_ref, added_ref, chain_first_ref, exit_ref, pull_ref,
                chain_last_ref, dv_ref, db_ref, dc_ref, dstep_ref, dcum_ref, enter_ref, leave_ref,
                step_ref, chain_ref, dv_out, db_out, dc_out, dstep_out, dlog_out, dskip_out):
    enter, leave, step = enter_ref[...], leave_ref[...], step_ref[...]
    heads = enter.shape[1]
    wide = 2 * P_SIZE
    lane = lax.broadcasted_iota(jnp.int32, (CH, wide), 1)
    low_lanes = lane < P_SIZE
    from_lane = lax.broadcasted_iota(jnp.int32, (wide, wide), 0)
    to_head = lax.broadcasted_iota(jnp.int32, (wide, wide), 1)
    leave_w = leave * step
    d_leave = jnp.zeros((CH, wide), f32)
    d_enter = jnp.zeros((CH, wide), f32)
    d_chain = jnp.zeros((8, wide), f32)
    d_skip = jnp.zeros((8, wide), f32)
    last_span = pl.program_id(0) == pl.num_programs(0) - 1
    d_b, d_c = db_ref[...], dc_ref[...]
    b_low, c_low = b_ref[...], c_ref[...]

    def summed(array, pick):
        high, rest = halves_of(array)
        return jnp.dot(high, pick, preferred_element_type=f32) + jnp.dot(
            rest, pick, preferred_element_type=f32
        )

    def crossed(one, two):
        one_high, one_rest = halves_of(one)
        two_high, two_rest = halves_of(two)
        return (
            inner_product(one_high, two_high)
            + inner_product(one_high, two_rest)
            + inner_product(one_rest, two_high)
        )

    for pair in range(heads // 2):
        lanes = pl.ds(pair * wide, wide)
        pick = (to_head == 2 * pair + from_lane // P_SIZE).astype(f32).astype(bf16)
        values = v_ref[:, lanes].astype(f32)
        grads = g_ref[:, lanes].astype(f32)
        states = entry_state(first_ref, added_ref, chain_first_ref, lanes)
        nexts = exit_ref[:, lanes]
        nexts = jnp.where(last_span, nexts, chain_last_ref[:, lanes] * nexts + pull_ref[:, lanes])
        leave_pair = pair_columns(leave_w, pair, low_lanes)
        b_pull = exact_dot(b_low, nexts)
        dv_out[:, lanes] = dv_ref[:, lanes] + leave_pair * b_pull
        d_leave = d_leave + summed(values * b_pull, pick)
        d_b = d_b + crossed(values * leave_pair, nexts)
        d_enter = d_enter + summed(grads * exact_dot(c_low, states), pick)
        d_c = d_c + crossed(pair_columns(enter, pair, low_lanes) * grads, states)
        column = jnp.sum(nexts * states, 0, keepdims=True)
        d_chain = d_chain + summed(jnp.broadcast_to(column, (8, wide)), pick)
        column = jnp.sum(grads * values, 0, keepdims=True)
        d_skip = d_skip + summed(jnp.broadcast_to(column, (8, wide)), pick)
    dskip_out[0] = d_skip
    db_out[...] = d_b
    dc_out[...] = d_c
    d_leave, d_enter, d_chain = d_leave[:, :heads], d_enter[:, :heads], d_chain[:1, :heads]
    dstep_out[...] = dstep_ref[...].T + d_leave * leave
    pulled = d_leave * leave_w
    d_cum = dcum_ref[...].T - pulled + d_enter * enter
    at_or_after = (
        lax.broadcasted_iota(jnp.int32, (CH, CH), 0) <= lax.broadcasted_iota(jnp.int32, (CH, CH), 1)
    ).astype(f32)
    last = jnp.sum(pulled, 0, keepdims=True) + d_chain * chain_ref[0]
    dlog_out[...] = jnp.dot(at_or_after, d_cum, precision=highest) + last


def late(values, grads, b_rows, c_rows, first, added, chain_first, last, pull, chain_last, dv, db, dc,
         d_step_t, d_cum_t, enter, leave, step, chained):
    rows, width = grads.shape
    heads = width // P_SIZE
    wide = pl.BlockSpec((CH, width), lambda s: (s, 0))
    group = pl.BlockSpec((CH, N), lambda s: (s, 0))
    state = pl.BlockSpec((N, width), lambda s: (0, 0))
    row = pl.BlockSpec((1, width), lambda s: (0, 0))
    turned = pl.BlockSpec((heads, CH), lambda s: (0, s))
    thin = pl.BlockSpec((CH, heads), lambda s: (s, 0))
    one = pl.BlockSpec((1, 1, heads), lambda s: (s, 0, 0))
    return pl.pallas_call(
        late_kernel,
        grid=(rows // CH,),
        in_specs=[wide, wide, group, group, state, state, row, state, state, row, wide, group, group,
                  turned, turned, thin, thin, thin, one],
        out_specs=[wide, group, group, thin, thin,
                   pl.BlockSpec((1, 8, 2 * P_SIZE), lambda s: (s, 0, 0))],
        out_shape=[
            jax.ShapeDtypeStruct((rows, width), f32),
            jax.ShapeDtypeStruct((rows, N), f32),
            jax.ShapeDtypeStruct((rows, N), f32),
            jax.ShapeDtypeStruct((rows, heads), f32),
            jax.ShapeDtypeStruct((rows, heads), f32),
            jax.ShapeDtypeStruct((rows // CH, 8, 2 * P_SIZE), f32),
        ],
        name="late",
    )(values, grads, b_rows, c_rows, first, added, chain_first, last, pull, chain_last, dv, db, dc,
      d_step_t, d_cum_t, enter, leave, step, chained[:, None])


def span_kernel(cum_ref, step_ref, seg_row_ref, seg_col_ref, b_ref, c_ref, v_ref, skip_ref, y_ref,
                scores_ref, bias_ref):
    @pl.when(pl.program_id(1) == 0)
    def _():
        scores_ref[...] = inner_product(c_ref[...], b_ref[...])
        bias_ref[...] = masked_bias(seg_row_ref[...], seg_col_ref[...])

    cum_rows = cum_ref[...]
    cum_cols = cum_rows.T
    step_rows = step_ref[...]
    low_lanes = lax.broadcasted_iota(jnp.int32, (CH, 2 * P_SIZE), 1) < P_SIZE
    for pair in range(HB // 2):
        lanes = pl.ds(pair * 2 * P_SIZE, 2 * P_SIZE)
        v_pair = v_ref[:, lanes]
        both = []
        for h in (2 * pair, 2 * pair + 1):
            decay = jnp.exp(cum_cols[:, h : h + 1] - cum_rows[h : h + 1, :] + bias_ref[...])
            mixing = (scores_ref[...] * decay * step_rows[h : h + 1, :]).astype(bf16)
            both.append(jnp.dot(mixing, v_pair, preferred_element_type=f32))
        y_ref[:, lanes] = (
            jnp.where(low_lanes, both[0], both[1]) + skip_ref[:, lanes] * v_pair.astype(f32)
        )


def span_outputs(cum_t, step_t, seg_row, seg_col, b_rows, c_rows, values, skip_row):
    rows, width = values.shape[0], skip_row.shape[1]
    wide = HB * P_SIZE
    return pl.pallas_call(
        span_kernel,
        grid=(rows // CH, width // wide),
        in_specs=[
            pl.BlockSpec((HB, CH), lambda s, g: (g, s)),
            pl.BlockSpec((HB, CH), lambda s, g: (g, s)),
            pl.BlockSpec((1, CH), lambda s, g: (0, s)),
            pl.BlockSpec((CH, 1), lambda s, g: (s, 0)),
            pl.BlockSpec((CH, N), lambda s, g: (s, 0)),
            pl.BlockSpec((CH, N), lambda s, g: (s, 0)),
            pl.BlockSpec((CH, wide), lambda s, g: (s, g)),
            pl.BlockSpec((1, wide), lambda s, g: (0, g)),
        ],
        out_specs=pl.BlockSpec((CH, wide), lambda s, g: (s, g)),
        out_shape=jax.ShapeDtypeStruct((rows, width), f32),
        scratch_shapes=[pltpu.VMEM((CH, CH), f32), pltpu.VMEM((CH, CH), f32)],
        name="span_outputs",
    )(cum_t, step_t, seg_row, seg_col, b_rows, c_rows, values, skip_row)


def span_back_kernel(cum_ref, step_ref, seg_row_ref, seg_col_ref, b_ref, c_ref, v_ref, skip_ref, g_ref,
                     dv_ref, dstep_ref, dcum_ref, db_ref, dc_ref, scores_ref, bias_ref, total_ref):
    @pl.when(pl.program_id(1) == 0)
    def _():
        scores_ref[...] = inner_product(c_ref[...], b_ref[...])
        bias_ref[...] = masked_bias(seg_row_ref[...], seg_col_ref[...])
        total_ref[...] = jnp.zeros_like(total_ref)

    cum_rows = cum_ref[...]
    cum_cols = cum_rows.T
    step_rows = step_ref[...]
    lane = lax.broadcasted_iota(jnp.int32, (CH, 2 * P_SIZE), 1)
    low_lanes = lane < P_SIZE
    row_sums = jnp.zeros((CH, 2 * P_SIZE), f32)
    zero = jnp.zeros((), bf16)
    for pair in range(HB // 2):
        lanes = pl.ds(pair * 2 * P_SIZE, 2 * P_SIZE)
        v_pair = v_ref[:, lanes]
        g_pair = g_ref[:, lanes]
        both = []
        for h in (2 * pair, 2 * pair + 1):
            step_row = step_rows[h : h + 1, :]
            scores = scores_ref[...]
            decay = jnp.exp(cum_cols[:, h : h + 1] - cum_rows[h : h + 1, :] + bias_ref[...])
            mixing_f = decay * step_row
            mixing = (scores * decay * step_row).astype(bf16)
            own = low_lanes if h % 2 == 0 else jnp.logical_not(low_lanes)
            d_mix = inner_product(jnp.where(own, g_pair, zero), v_pair)
            both.append(
                lax.dot_general(mixing, g_pair, (((0,), (0,)), ((), ())), preferred_element_type=f32)
            )
            total_ref[...] += d_mix * mixing_f
            weighted = d_mix * scores * decay
            column = jnp.sum(weighted, 0, keepdims=True)
            dstep_ref[h : h + 1, :] = column
            dcum_ref[h : h + 1, :] = -column * step_row
            row_sums = row_sums + jnp.where(
                lane == h, jnp.sum(weighted * step_row, 1, keepdims=True), 0.0
            )
        dv_ref[:, lanes] = (
            jnp.where(low_lanes, both[0], both[1]) + skip_ref[:, lanes] * g_pair.astype(f32)
        )
    dcum_ref[...] += row_sums.T[:HB, :]

    @pl.when(pl.program_id(1) == pl.num_programs(1) - 1)
    def _():
        total = total_ref[...]
        dc_ref[...] = jnp.dot(total, b_ref[...].astype(f32), precision=highest)
        db_ref[...] = jnp.dot(total.T, c_ref[...].astype(f32), precision=highest)


def span_backs(cum_t, step_t, seg_row, seg_col, b_rows, c_rows, values, skip_row, grads):
    rows, width = grads.shape
    wide = HB * P_SIZE
    heads = width // P_SIZE
    return pl.pallas_call(
        span_back_kernel,
        grid=(rows // CH, width // wide),
        in_specs=[
            pl.BlockSpec((HB, CH), lambda s, g: (g, s)),
            pl.BlockSpec((HB, CH), lambda s, g: (g, s)),
            pl.BlockSpec((1, CH), lambda s, g: (0, s)),
            pl.BlockSpec((CH, 1), lambda s, g: (s, 0)),
            pl.BlockSpec((CH, N), lambda s, g: (s, 0)),
            pl.BlockSpec((CH, N), lambda s, g: (s, 0)),
            pl.BlockSpec((CH, wide), lambda s, g: (s, g)),
            pl.BlockSpec((1, wide), lambda s, g: (0, g)),
            pl.BlockSpec((CH, wide), lambda s, g: (s, g)),
        ],
        out_specs=[
            pl.BlockSpec((CH, wide), lambda s, g: (s, g)),
            pl.BlockSpec((HB, CH), lambda s, g: (g, s)),
            pl.BlockSpec((HB, CH), lambda s, g: (g, s)),
            pl.BlockSpec((CH, N), lambda s, g: (s, 0)),
            pl.BlockSpec((CH, N), lambda s, g: (s, 0)),
        ],
        out_shape=[
            jax.ShapeDtypeStruct((rows, width), f32),
            jax.ShapeDtypeStruct((heads, rows), f32),
            jax.ShapeDtypeStruct((heads, rows), f32),
            jax.ShapeDtypeStruct((rows, N), f32),
            jax.ShapeDtypeStruct((rows, N), f32),
        ],
        scratch_shapes=[pltpu.VMEM((CH, CH), f32)] * 3,
        name="span_backs",
    )(cum_t, step_t, seg_row, seg_col, b_rows, c_rows, values, skip_row, grads)


def shards(
    tokens,
    cotangent,
    seg_ids,
    carry_flags,
    inner_weight,
    inner_velocity,
    inner_average,
    groups_weight,
    groups_velocity,
    groups_average,
    stepper_weight,
    stepper_velocity,
    stepper_average,
    outer_weight,
    outer_velocity,
    outer_average,
    filters_weight,
    filters_velocity,
    filters_average,
    probes_weight,
    probes_velocity,
    probes_average,
    prenorm_weight,
    prenorm_velocity,
    prenorm_average,
    postnorm_weight,
    postnorm_velocity,
    postnorm_average,
    heads_weight,
    heads_velocity,
    heads_average,
):
    local_rows = tokens.shape[0]
    share = tokens.shape[1]
    value_width = filters_weight.shape[1]
    group_width = probes_weight.shape[1]
    heads_local = heads_weight.shape[1]
    span_count = local_rows // CH
    edge_count = KC - 1
    conv_width = value_width + group_width
    pad_heads = group_width - heads_local
    upper = lax.axis_index(HEAD) == 1
    seq_count = lax.axis_size(SEQ)

    shard_a = jnp.concatenate(
        [
            inner_weight[:, 1],
            groups_weight,
            jnp.pad(stepper_weight, ((0, 0), (0, pad_heads))),
        ],
        1,
    ).astype(bf16)
    cut = shard_a.shape[1] // 2
    orders = bit_orders(SEQ)
    far = orders[0][:1:-1]
    near = [order[1::-1] for order in orders]
    begun = gather_rows(shard_a, SEQ, far[:1])
    other = swap(begun, SEQ, 1 << far[1]) if len(far) > 1 else begun
    edge_own = shifted(tokens[local_rows - 8 :], SEQ, 1)
    tokens_ext = jnp.concatenate([edge_own, tokens], 0)
    rows_ext = side_by_side(tokens_ext, swap(tokens_ext, HEAD, 1), upper)
    rows_in = rows_ext[8:]
    rows_ext = rows_ext.astype(f32)
    normed_ext = (
        rows_ext
        * lax.rsqrt(jnp.mean(rows_ext * rows_ext, -1, keepdims=True) + epsilon)
        * prenorm_weight
    ).astype(bf16)
    held_bc = jnp.concatenate(
        [inner_weight[:, 0].astype(bf16), outer_weight.astype(bf16).T], 1
    )
    other, held_bc, normed_ext = lax.optimization_barrier((other, held_bc, normed_ext))
    if len(far) > 1:
        begun = assemble(begun, other, SEQ, far[1], far[:1])
        begun = gather_rows(begun, SEQ, far[2:], far[:2])
    held_a = [begun[:, :cut], begun[:, cut:]]
    other_a = [swap(held_a[k], SEQ, 1 << near[k][0]) for k in range(2)]
    held_bc = after(held_bc, begun)
    other_bc = swap(held_bc, SEQ, 1 << far[0])
    grads_in = side_by_side(cotangent, swap(cotangent, HEAD, 1), upper)
    held_a = [assemble(held_a[k], other_a[k], SEQ, near[k][0], far) for k in range(2)]
    other_a = [swap(held_a[k], SEQ, 1 << near[k][1]) for k in range(2)]
    normed_ext = after(normed_ext, held_a)
    ext_sides = [
        [pick_columns(normed_ext, SEQ, order[0], other) for other in (False, True)]
        for order in orders
    ]
    normed_sides = [[side[8:] for side in sides] for sides in ext_sides]
    held_bc = assemble(held_bc, after(other_bc, held_a), SEQ, far[0], ())
    if len(far) > 1:
        other_bc = swap(held_bc, SEQ, 1 << far[1])
    grads_sides = [pick_columns(grads_in, SEQ, orders[1][0], other) for other in (False, True)]
    own_a = [
        jnp.dot(ext_sides[k][0], held_a[k], preferred_element_type=f32) for k in range(2)
    ]
    other_a, own_a, grads_sides = lax.optimization_barrier((other_a, own_a, grads_sides))
    raw_a = jnp.concatenate(
        lax.optimization_barrier(
            [
                own_a[k] + jnp.dot(ext_sides[k][1], other_a[k], preferred_element_type=f32)
                for k in range(2)
            ]
        ),
        1,
    )
    rows_float = rows_in.astype(f32)
    inverse = lax.rsqrt(jnp.mean(rows_float * rows_float, -1, keepdims=True) + epsilon)
    unit_rows = rows_float * inverse
    normed = (unit_rows * prenorm_weight).astype(bf16)

    other_bc, held_bc, raw_a = lax.optimization_barrier((other_bc, held_bc, raw_a))
    if len(far) > 1:
        held_bc = assemble(held_bc, other_bc, SEQ, far[1], far[:1])
        held_bc = gather_rows(held_bc, SEQ, far[2:], far[:2])
    held_bc = [held_bc[:, :value_width], held_bc[:, value_width:]]
    other_bc = [swap(held_bc[k], SEQ, 1 << near[k][0]) for k in range(2)]
    raw_a = after(raw_a, held_bc)
    step_raw = raw_a[8:, conv_width : conv_width + heads_local]
    extended = lax.reduce_precision(raw_a[8 - edge_count :, :conv_width], 8, 7)
    masks = tap_masks(seg_ids, carry_flags, CH, KC)
    tap_rows = jnp.concatenate([filters_weight, probes_weight], 1)
    conv_out = conv_apply(extended, tap_rows, masks, KC)
    activated = jax.nn.silu(conv_out).astype(bf16)
    own_group = activated[:, value_width:]
    other_group = swap(own_group, HEAD, 1)
    b_rows = jnp.where(upper, other_group, own_group)
    c_rows = jnp.where(upper, own_group, other_group)

    step_pre = step_raw + heads_weight[0]
    step_size = jax.nn.softplus(step_pre)
    decay_rate = -jnp.exp(heads_weight[1])
    log_decay = step_size * decay_rate
    skip_row = expand(heads_weight[2:3])
    seg_spans = seg_ids.reshape(span_count, CH)
    cumulative, entering, leaving, chained = span_edges(
        log_decay.reshape(span_count, CH, heads_local), seg_spans, carry_flags
    )
    cum_t = cumulative.reshape(local_rows, heads_local).T
    step_t = step_size.T
    seg_row = seg_ids.reshape(1, local_rows)
    seg_col = seg_ids.reshape(local_rows, 1)
    enter_wide = expand(entering.reshape(local_rows, heads_local))
    leave_w = leaving.reshape(local_rows, heads_local) * step_size
    leave_wide = expand(leave_w)
    chain_wide = expand(chained)
    factor = jnp.prod(chained, 0)
    b_float = b_rows.astype(f32)
    c_float = c_rows.astype(f32)
    b_spans = b_float.reshape(span_count, CH, N)
    c_spans = c_float.reshape(span_count, CH, N)

    def by_span(array):
        return array.reshape((span_count, CH) + array.shape[1:])

    values_float = activated[:, :value_width].astype(f32)
    local_states = jnp.einsum(
        "cjn,cjw->cnw", b_spans, by_span(values_float * leave_wide), precision=highest
    )
    summary = local_states[0]
    for span in range(1, span_count):
        summary = chain_wide[span] * summary + local_states[span]
    sent_parts = jnp.concatenate(
        [summary, jnp.broadcast_to(jnp.pad(factor, (0, N - heads_local))[None], (N, N))], 1
    )
    pieces = parts_out(sent_parts, SEQ)
    other_bc = after(other_bc, sent_parts)
    held_bc = [assemble(held_bc[k], other_bc[k], SEQ, near[k][0], far) for k in range(2)]
    other_bc = [swap(held_bc[k], SEQ, 1 << near[k][1]) for k in range(2)]
    local_out = span_outputs(
        cum_t, step_t, seg_row, seg_col, b_rows, c_rows, after(activated, held_bc), skip_row
    )
    pieces = after(pieces, local_out)
    factors = expand(pieces[:, 0, value_width : value_width + heads_local])[:, None]
    walked, entered = walked_in(pieces, factors, SEQ, False)
    sides_bc = [normed_sides[0], grads_sides]
    own_bc = [
        jnp.dot(sides_bc[k][0], held_bc[k], preferred_element_type=f32) for k in range(2)
    ]
    entered, own_bc = lax.optimization_barrier((entered, own_bc))
    gate_pre, d_mixed = [
        own_bc[k] + jnp.dot(sides_bc[k][1], other_bc[k], preferred_element_type=f32)
        for k in range(2)
    ]
    enter_rows = entering.reshape(local_rows, heads_local)
    gain_row = postnorm_weight[None]
    carried = (entered, local_states[0], chain_wide[:1])
    middle_args = (local_out, gate_pre, d_mixed, c_rows) + carried + (gain_row, enter_rows)
    row_own = row_sums(*middle_args)
    row_other = swap(row_own, HEAD, 1)
    mixed, d_ssd, d_gate, d_post, pull_total, pull_last = middle(
        *middle_args, row_own, row_other
    )
    d_post = d_post[0]

    def split_features(array):
        lower_half, upper_half = array[:, :share], array[:, share:]
        return (
            jnp.where(upper, upper_half, lower_half),
            jnp.where(upper, lower_half, upper_half),
        )

    def own_features(array):
        own, other = split_features(array)
        return own + swap(other, HEAD, 1)

    def back_product(grads, weights):
        return lax.dot_general(
            grads, weights, (((1,), (1,)), ((), ())), preferred_element_type=f32
        )

    pull_pieces = parts_out(pull_total, SEQ)
    mixed, d_gate = after((mixed, d_gate), pull_total)
    order_c, order_b = orders[1], orders[0]
    half = value_width // 2
    firsts = [1 << order_c[0], 1 << order_b[0]]
    lefts = [grads_sides, normed_sides[0]]
    sent_one = [
        token_product(side[1], grad[:, :half]).astype(bf16)
        for side, grad in zip(lefts, (mixed, d_gate))
    ]
    got_one = [swap(sent, SEQ, mask) for sent, mask in zip(sent_one, firsts)]
    d_ssd = after(d_ssd, sent_one)
    dv_local, d_step_t, d_cum_t, db_local, dc_local = span_backs(
        cum_t, step_t, seg_row, seg_col, b_rows, c_rows, activated, skip_row, d_ssd
    )
    pull_pieces, dv_local = lax.optimization_barrier((pull_pieces, dv_local))
    walked, running = walked_in(pull_pieces, factors, SEQ, True)
    mixed, d_gate = after((mixed, d_gate), walked)
    sent_two = [
        token_product(side[1], grad[:, half:]).astype(bf16)
        for side, grad in zip(lefts, (mixed, d_gate))
    ]
    got_two = [swap(sent, SEQ, mask) for sent, mask in zip(sent_two, firsts)]
    kept_bc = [token_product(side[0], grad) for side, grad in zip(lefts, (mixed, d_gate))]
    running = after(running, kept_bc, sent_two)
    leave_rows = leaving.reshape(local_rows, heads_local)
    d_values, d_b_rows, d_c_rows, d_step, d_log, d_skip = late(
        activated, d_ssd, b_rows, c_rows, *carried, running, pull_last, chain_wide[1:],
        dv_local, db_local, dc_local, d_step_t, d_cum_t, enter_rows, leave_rows, step_size, chained,
    )
    d_skip = jnp.sum(d_skip[:, 0, :heads_local], 0)
    d_step_all = d_step + d_log * decay_rate
    d_alog = jnp.sum(d_log * step_size, 0) * decay_rate
    d_pre = d_step_all * jax.nn.sigmoid(step_pre)
    d_bias = jnp.sum(d_pre, 0)
    d_step_low = d_pre.astype(bf16)

    group_share = jnp.where(upper, d_c_rows, d_b_rows) + swap(
        jnp.where(upper, d_b_rows, d_c_rows), HEAD, 1
    )
    head_grad = jnp.concatenate([d_values[:8], group_share[:8]], 1) * silu_slope(conv_out[:8])
    head_ext = sum(
        jnp.pad(
            tap_rows[lagged] * masks[lagged - 1][:8, None] * head_grad,
            ((edge_count - lagged, lagged), (0, 0)),
        )
        for lagged in range(1, KC)
    )[:edge_count]
    from_next = shifted(head_ext, SEQ, -1)
    got_one, got_two, kept_bc = after((got_one, got_two, kept_bc), head_ext)
    held_bc_grad = [
        kept + jnp.concatenate([one, two], 1).astype(f32)
        for kept, one, two in zip(kept_bc, got_one, got_two)
    ]
    seconds = [order_c[1:], order_b[1:]]
    kept_bc, sent_bc = zip(
        *[sides_of(h, SEQ, left[0], left) for h, left in zip(held_bc_grad, seconds)]
    )
    got_bc = [swap(sent, SEQ, 1 << left[0]) for sent, left in zip(sent_bc, seconds)]
    d_values, group_share = after((d_values, group_share), sent_bc)
    d_conv = jnp.concatenate([d_values, group_share], 1) * silu_slope(conv_out)
    d_taps, ext_grad = conv_backward(extended, tap_rows, masks, d_conv, KC)
    from_next = after(from_next, sent_bc)
    rest = orders[0][2:]
    d_conv_in = ext_grad[edge_count:] + jnp.pad(from_next, ((local_rows - edge_count, 0), (0, 0)))
    grads_a = jnp.concatenate(
        [d_conv_in.astype(bf16), jnp.pad(d_step_low, ((0, 0), (0, pad_heads)))], 1
    )
    parts_a = [grads_a[:, :cut], grads_a[:, cut:]]
    sent_a = [token_product(normed_sides[k][1], parts_a[k]).astype(bf16) for k in range(2)]
    got_a = [swap(sent_a[k], SEQ, 1 << orders[k][0]) for k in range(2)]
    parts_a, held_a, other_a, held_bc, other_bc, got_bc = after(
        (parts_a, held_a, other_a, held_bc, other_bc, got_bc), sent_a
    )
    full_a = [
        assemble(held_a[k], other_a[k], SEQ, near[k][1], far + near[k][:1]) for k in range(2)
    ]
    full_b, full_c = [
        assemble(held_bc[k], other_bc[k], SEQ, near[k][1], far + near[k][:1]) for k in range(2)
    ]
    heads_flat = jnp.concatenate([d_bias, d_alog, d_skip])
    small = jnp.concatenate(
        [
            d_taps,
            jnp.pad(d_post, (0, group_width))[None],
            jnp.pad(heads_flat, (0, conv_width - 3 * heads_local))[None],
        ],
        0,
    )
    small = butterfly_sum(after(small, sent_a), SEQ, orders[0][2:])
    d_normed_own, d_normed_other = split_features(
        back_product(d_gate, full_b)
        + back_product(parts_a[0], full_a[0])
        + back_product(parts_a[1], full_a[1])
    )
    d_normed_got = swap(d_normed_other, HEAD, 1)
    held_bc_grad = [k + g.astype(f32) for k, g in zip(kept_bc, got_bc)]
    kept_bc, sent_bc = zip(*[sides_of(h, SEQ, rest[0], rest) for h in held_bc_grad])
    got_bc = [swap(sent, SEQ, 1 << rest[0]) for sent in sent_bc]
    got_bc = after(got_bc, d_normed_other)
    held_bc_grad = [k + g.astype(f32) for k, g in zip(kept_bc, got_bc)]
    if len(rest) > 1:
        kept_bc, sent_bc = zip(*[sides_of(h, SEQ, rest[1], rest[1:]) for h in held_bc_grad])
        got_bc = [swap(sent, SEQ, 1 << rest[1]) for sent in sent_bc]
    kept_a = [token_product(normed_sides[k][0], parts_a[k]) for k in range(2)]
    kept_a, got_a = after((kept_a, got_a), sent_bc, d_normed_other)
    kept_a, sent_a = zip(
        *[
            sides_of(kept_a[k] + got_a[k].astype(f32), SEQ, orders[k][1], orders[k][1:])
            for k in range(2)
        ]
    )
    got_a = [swap(sent_a[k], SEQ, 1 << orders[k][1]) for k in range(2)]
    d_normed_own, d_normed_got, mixed, full_c = after(
        (d_normed_own, d_normed_got, mixed, full_c), sent_a
    )
    d_normed = d_normed_own + d_normed_got
    own_unit = jnp.where(upper, unit_rows[:, share:], unit_rows[:, :share])
    own_gain = jnp.where(upper, prenorm_weight[share:], prenorm_weight[:share])
    own_rows = tokens.astype(f32)
    d_prenorm = jnp.sum(d_normed * own_unit, 0)
    d_unit_in = d_normed * own_gain
    mean_own = jnp.sum(d_unit_in * own_rows, -1)
    row_mean = ((mean_own + swap(mean_own, HEAD, 1)) / D)[:, None]
    input_gradient = (
        cotangent.astype(f32) + inverse * d_unit_in - own_rows * inverse**3 * row_mean
    )

    held_a = jnp.concatenate([k + g.astype(f32) for k, g in zip(kept_a, got_a)], 1)
    kept_a, sent_a = sides_of(held_a, SEQ, rest[0], rest)
    got_a = swap(sent_a, SEQ, 1 << rest[0])
    small, d_prenorm = after((small, d_prenorm[None]), sent_a)
    small = butterfly_sum(small, SEQ, orders[0][:2])
    d_prenorm = butterfly_sum(d_prenorm, SEQ, orders[0][:2])
    projected = own_features(back_product(mixed, full_c))
    output = (tokens.astype(f32) + projected).astype(bf16)
    held_a = kept_a + got_a.astype(f32)
    kept_a, sent_a = sides_of(held_a, SEQ, rest[1], rest[1:])
    got_a = swap(sent_a, SEQ, 1 << rest[1])
    prenorm_own = butterfly_sum(after(d_prenorm, sent_a), SEQ, rest)
    got_bc = after(got_bc, sent_a)
    if len(rest) > 1:
        held_bc_grad = [k + g.astype(f32) for k, g in zip(kept_bc, got_bc)]
    outer_grad, gate_grad = [scatter_rows(h, SEQ, rest[2:], rest[2:]) for h in held_bc_grad]
    outer_grad = outer_grad.T
    got_a = after(got_a, output, input_gradient)
    rest_grad = scatter_rows(kept_a + got_a.astype(f32), SEQ, rest[2:], rest[2:])
    filters_grad = small[: KC + 1, :value_width]
    probes_grad = small[: KC + 1, value_width:]
    postnorm_grad = small[KC + 1, :value_width]
    prenorm_grad = side_by_side(prenorm_own, swap(prenorm_own, HEAD, 1), upper)[0]
    heads_grad = small[KC + 2, : 3 * heads_local].reshape(3, heads_local)

    groups_grad = rest_grad[:, value_width:conv_width]
    stepper_grad = rest_grad[:, conv_width : conv_width + heads_local]
    root = math.sqrt(local_rows * seq_count)
    inner_new = update_inner(
        inner_weight, inner_velocity, inner_average, gate_grad, rest_grad, D ** (-0.5) / root
    )
    groups_new = apply_update(
        groups_weight, groups_velocity, groups_average, groups_grad, D ** (-0.5) / root
    )
    stepper_new = apply_update(
        stepper_weight, stepper_velocity, stepper_average, stepper_grad, (4 * D) ** (-0.5) / root
    )
    outer_new = apply_update(
        outer_weight, outer_velocity, outer_average, outer_grad, DI ** (-0.5) / root
    )
    filters_new = apply_update(
        filters_weight, filters_velocity, filters_average, filters_grad, 0.5 / root
    )
    probes_new = apply_update(
        probes_weight, probes_velocity, probes_average, probes_grad, 0.5 / root
    )
    prenorm_new = apply_update(
        prenorm_weight, prenorm_velocity, prenorm_average, prenorm_grad, 0.1 / root
    )
    postnorm_new = apply_update(
        postnorm_weight, postnorm_velocity, postnorm_average, postnorm_grad, 0.1 / root
    )
    heads_new = apply_update(heads_weight, heads_velocity, heads_average, heads_grad, 0.5 / root)
    return (
        output,
        input_gradient,
        inner_new[0],
        inner_new[1],
        inner_new[2],
        inner_new[3],
        groups_new[0],
        groups_new[1],
        groups_new[2],
        groups_new[3],
        stepper_new[0],
        stepper_new[1],
        stepper_new[2],
        stepper_new[3],
        outer_new[0],
        outer_new[1],
        outer_new[2],
        outer_new[3],
        filters_new[0],
        filters_new[1],
        filters_new[2],
        filters_new[3],
        probes_new[0],
        probes_new[1],
        probes_new[2],
        probes_new[3],
        prenorm_new[0],
        prenorm_new[1],
        prenorm_new[2],
        prenorm_new[3],
        postnorm_new[0],
        postnorm_new[1],
        postnorm_new[2],
        postnorm_new[3],
        heads_new[0],
        heads_new[1],
        heads_new[2],
        heads_new[3],
    )


def solution(mesh):
    return jax.shard_map(
        shards,
        mesh=mesh,
        in_specs=(
            P(SEQ, HEAD),
            P(SEQ, HEAD),
            P(SEQ),
            P(SEQ),
            P(SEQ, None, HEAD),
            P(SEQ, None, HEAD),
            P(SEQ, None, HEAD),
            P(SEQ, HEAD),
            P(SEQ, HEAD),
            P(SEQ, HEAD),
            P(SEQ, HEAD),
            P(SEQ, HEAD),
            P(SEQ, HEAD),
            P(HEAD, SEQ),
            P(HEAD, SEQ),
            P(HEAD, SEQ),
            P(None, HEAD),
            P(None, HEAD),
            P(None, HEAD),
            P(None, HEAD),
            P(None, HEAD),
            P(None, HEAD),
            P(),
            P(),
            P(),
            P(HEAD),
            P(HEAD),
            P(HEAD),
            P(None, HEAD),
            P(None, HEAD),
            P(None, HEAD),
        ),
        out_specs=(
            P(SEQ, HEAD),
            P(SEQ, HEAD),
            P(SEQ, None, HEAD),
            P(SEQ, None, HEAD),
            P(SEQ, None, HEAD),
            P(SEQ, None, HEAD),
            P(SEQ, HEAD),
            P(SEQ, HEAD),
            P(SEQ, HEAD),
            P(SEQ, HEAD),
            P(SEQ, HEAD),
            P(SEQ, HEAD),
            P(SEQ, HEAD),
            P(SEQ, HEAD),
            P(HEAD, SEQ),
            P(HEAD, SEQ),
            P(HEAD, SEQ),
            P(HEAD, SEQ),
            P(None, HEAD),
            P(None, HEAD),
            P(None, HEAD),
            P(None, HEAD),
            P(None, HEAD),
            P(None, HEAD),
            P(None, HEAD),
            P(None, HEAD),
            P(),
            P(),
            P(),
            P(),
            P(HEAD),
            P(HEAD),
            P(HEAD),
            P(HEAD),
            P(None, HEAD),
            P(None, HEAD),
            P(None, HEAD),
            P(None, HEAD),
        ),
        check_vma=False,
    )
```

profile of v0, /device:TPU:0, one launch (start us, length us, event | category | flops | bytes accessed | tf_op | source)
XLA Modules:
  0.0 513.8 jit_solution(6516181721632305187)
XLA Ops:
  1.6 5.0 collective-permute-start.2
  15.7 11.2 %collective-permute-done = bf16[96,1792]{1,0:T(8,128)(2,1)} collective-permute-done((bf16[96,1792]{1,0:T(8,128)(2,1)S(1)}, bf16[96,1792]{1,0:T(8,128)(2,1)}, u32[]{:S(2)}, u32[]{:S(2)}) %collective-permute-start) | collective-permute-done | bytes 344096 | tf_op jit(solution)/shard_map/ppermute | solution.py:38
  31.1 13.5 %collective-permute-done.1 = bf16[192,1792]{1,0:T(8,128)(2,1)S(1)} collective-permute-done((bf16[192,1792]{1,0:T(8,128)(2,1)S(1)}, bf16[192,1792]{1,0:T(8,128)(2,1)S(1)}, u32[]{:S(2)}, u32[]{:S(2)}) %collective-permute-start.1) | collective-permute-done | bytes 688160 | tf_op jit(solution)/shard_map/ppermute | solution.py:38
  54.9 7.0 %collective-permute-done.5 = bf16[384,896]{1,0:T(8,128)(2,1)} collective-permute-done((bf16[384,896]{1,0:T(8,128)(2,1)}, bf16[384,896]{1,0:T(8,128)(2,1)}, u32[]{:S(2)}, u32[]{:S(2)}) %collective-permute-start.5) | collective-permute-done | bytes 688160 | tf_op jit(solution)/shard_map/ppermute | solution.py:38
  70.9 9.6 %collective-permute-done.4 = bf16[96,3072]{1,0:T(8,128)(2,1)} collective-permute-done((bf16[96,3072]{1,0:T(8,128)(2,1)}, bf16[96,3072]{1,0:T(8,128)(2,1)}, u32[]{:S(2)}, u32[]{:S(2)}) %collective-permute-start.4) | collective-permute-done | bytes 589856 | tf_op jit(solution)/shard_map/ppermute | solution.py:38
  89.3 6.1 %collective-permute-done.9 = bf16[768,896]{1,0:T(8,128)(2,1)} collective-permute-done((bf16[768,896]{1,0:T(8,128)(2,1)}, bf16[768,896]{1,0:T(8,128)(2,1)}, u32[]{:S(2)}, u32[]{:S(2)}) %collective-permute-start.9) | collective-permute-done | bytes 1376288 | tf_op jit(solution)/shard_map/ppermute | solution.py:38
  101.3 7.7 %collective-permute-done.7 = bf16[192,3072]{1,0:T(8,128)(2,1)S(1)} collective-permute-done((bf16[192,3072]{1,0:T(8,128)(2,1)S(1)}, bf16[192,3072]{1,0:T(8,128)(2,1)S(1)}, u32[]{:S(2)}, u32[]{:S(2)}) %collective-permute-start.7) | collective-permute-done | bytes 1179680 | tf_op jit(solution)/shard_map/ppermute | solution.py:38
  114.7 4.7 multiply_convert_fusion
  127.8 6.8 %all-to-all-start = ((f32[16,8,1664]{2,1,0:T(8,128)}), f32[16,8,1664]{2,1,0:T(8,128)}, u32[]{:S(2)}, u32[]{:S(2)}) async-start(f32[16,8,1664]{2,1,0:T(8,128)} %pad_maximum_fusion.15), calls=%async_computation | async-start | bytes 1703936 | tf_op jit(solution)/shard_map/all_to_all | solution.py:195
  134.6 6.4 %collective-permute-done.12 = bf16[384,1536]{1,0:T(8,128)(2,1)} collective-permute-done((bf16[384,1536]{1,0:T(8,128)(2,1)}, bf16[384,1536]{1,0:T(8,128)(2,1)}, u32[]{:S(2)}, u32[]{:S(2)}) %collective-permute-start.12) | collective-permute-done | bytes 1179680 | tf_op jit(solution)/shard_map/ppermute | solution.py:38
  141.0 4.0 broadcast_select_fusion.9
  157.0 8.4 %span_outputs.1.refs_0_.all_refs_0_ = f32[512,1536]{1,0:T(8,128)} custom-call(f32[24,512]{1,0:T(8,128)} %bitcast.343, f32[24,512]{1,0:T(8,128)} %copy.186.step_ref, s32[1,512]{1,0:T(1,128)} %bitcast.345, s32[512,1]{1,0:T(8,128)} %copy.187.seg_col_ref, bf16[512,128]{1,0:T(8,128)(2,1)} %copy-done.31, ...), custom_call_target="tpu_custom_call" | custom-call | tf_op jit(solution)/shard_map/span_outputs/pallas_call | solution.py:500
  169.3 11.4 %all-to-all-start.1 = ((f32[16,8,1536]{2,1,0:T(8,128)}), f32[16,8,1536]{2,1,0:T(8,128)}, u32[]{:S(2)}, u32[]{:S(2)}) async-start(f32[16,8,1536]{2,1,0:T(8,128)} %walk.2), calls=%async_computation.1 | async-start | bytes 1572864 | tf_op jit(solution)/shard_map/all_to_all | solution.py:206
  185.5 4.8 fusion.68
  190.3 4.7 fusion.67
  195.0 16.2 %all-to-all-done.1 = f32[16,8,1536]{2,1,0:T(8,128)} async-done(((f32[16,8,1536]{2,1,0:T(8,128)}), f32[16,8,1536]{2,1,0:T(8,128)}, u32[]{:S(2)}, u32[]{:S(2)}) %all-to-all-start.1) | async-done | bytes 786464 | tf_op jit(solution)/shard_map/all_to_all | solution.py:206
  211.2 6.1 %convolution_add_fusion.refs_2_.all_refs_2_ = f32[512,1536]{1,0:T(8,128)} fusion(f32[512,1536]{1,0:T(8,128)} %fusion.68, bf16[512,768]{0,1:T(8,128)(2,1)} %bitcast.315, bf16[768,1536]{1,0:T(8,128)(2,1)} %collective-permute-done.15), kind=kOutput, calls=%fused_computation.24 | convolution fusion | flops 1208745984 | bytes 9437184 | tf_op jit(solution)/shard_map/dot_general | solution.py:789
  217.4 4.8 convolution_add_fusion.1.refs_1_.all_refs_1_
  222.2 6.5 %row_sums.1.all_refs_9_ = f32[512,128]{1,0:T(8,128)} custom-call(f32[512,1536]{1,0:T(8,128)} %span_outputs.1.refs_0_.all_refs_0_, f32[512,1536]{1,0:T(8,128)} %convolution_add_fusion.1.refs_1_.all_refs_1_, f32[512,1536]{1,0:T(8,128)} %convolution_add_fusion.refs_2_.all_refs_2_, bf16[512,128]{1,0:T(8,128)(2,1)} %get-tuple-element.462.c_ref.refs_3_.all_refs_3_, ...), custom_call_target="tpu_custom_call" | custom-call | tf_op jit(solution)/shard_map/row_sums/pallas_call | solution.py:311
  230.6 10.8 %middle.1 = (bf16[512,1536]{1,0:T(8,128)(2,1)}, bf16[512,1536]{1,0:T(8,128)(2,1)}, bf16[512,1536]{1,0:T(8,128)(2,1)}, f32[1,1536]{1,0:T(1,128)}, f32[128,1536]{1,0:T(8,128)}, /*index=5*/f32[128,1536]{1,0:T(8,128)}) custom-call(f32[512,1536]{1,0:T(8,128)} %span_outputs.1.refs_0_.all_refs_0_, f32[512,1536]{1,0:T(8,128)} %convolution_add_fusion.1.refs_1_.all_refs_1_, ...), custom_call_target="tpu_custom_call" | custom-call | tf_op jit(solution)/shard_map/middle/pallas_call | solution.py:357
  241.4 9.5 %all-to-all-start.2 = ((f32[16,8,1536]{2,1,0:T(8,128)}), f32[16,8,1536]{2,1,0:T(8,128)}, u32[]{:S(2)}, u32[]{:S(2)}) async-start(f32[16,8,1536]{2,1,0:T(8,128)} %bitcast.334), calls=%async_computation.2 | async-start | bytes 1572864 | tf_op jit(solution)/shard_map/all_to_all | solution.py:195
  262.5 19.2 %span_backs.1 = (f32[512,1536]{1,0:T(8,128)}, f32[24,512]{1,0:T(8,128)}, f32[24,512]{1,0:T(8,128)}, f32[512,128]{1,0:T(8,128)}, f32[512,128]{1,0:T(8,128)}) custom-call(f32[24,512]{1,0:T(8,128)} %bitcast.344, f32[24,512]{1,0:T(8,128)} %copy.186.step_ref, s32[1,512]{1,0:T(1,128)} %bitcast.346, s32[512,1]{1,0:T(8,128)} %copy.187.seg_col_ref, ...), custom_call_target="tpu_custom_call" | custom-call | tf_op jit(solution)/shard_map/span_backs/pallas_call | solution.py:575
  283.9 7.0 %all-to-all-start.3 = ((f32[16,8,1536]{2,1,0:T(8,128)}), f32[16,8,1536]{2,1,0:T(8,128)}, u32[]{:S(2)}, u32[]{:S(2)}) async-start(f32[16,8,1536]{2,1,0:T(8,128)} %walk.3), calls=%async_computation.3 | async-start | bytes 1572864 | tf_op jit(solution)/shard_map/all_to_all | solution.py:206
  310.7 14.3 %late.1 = (f32[512,1536]{1,0:T(8,128)}, f32[512,128]{1,0:T(8,128)}, f32[512,128]{1,0:T(8,128)}, f32[512,24]{1,0:T(8,128)}, f32[512,24]{1,0:T(8,128)}, /*index=5*/f32[2,8,128]{2,1,0:T(8,128)}) custom-call(bf16[512,1664]{1,0:T(8,128)(2,1)} %copy-done, bf16[512,1536]{1,0:T(8,128)(2,1)} %get-tuple-element.161.g_ref, bf16[512,128]{1,0:T(8,128)(2,1)} %copy-done.31, ...), custom_call_target="tpu_custom_call" | custom-call | tf_op jit(solution)/shard_map/late/pallas_call | solution.py:453
  334.6 19.1 %collective-permute-done.21 = bf16[768,768]{1,0:T(8,128)(2,1)} collective-permute-done((bf16[768,768]{1,0:T(8,128)(2,1)}, bf16[768,768]{1,0:T(8,128)(2,1)}, u32[]{:S(2)}, u32[]{:S(2)}) %collective-permute-start.21) | collective-permute-done | bytes 1179680 | tf_op jit(solution)/shard_map/ppermute | solution.py:38
  370.9 4.5 broadcast_multiply_fusion
  375.6 5.1 fusion.1
  403.8 4.3 fusion.71
  433.8 10.6 %collective-permute-done.34 = bf16[384,896]{1,0:T(8,128)(2,1)S(1)} collective-permute-done((bf16[384,896]{1,0:T(8,128)(2,1)S(1)}, bf16[384,896]{1,0:T(8,128)(2,1)S(1)}, u32[]{:S(2)}, u32[]{:S(2)}) %collective-permute-start.34) | collective-permute-done | bytes 688160 | tf_op jit(solution)/shard_map/ppermute | solution.py:38
  466.9 8.4 %collective-permute-done.36 = bf16[192,1792]{1,0:T(8,128)(2,1)} collective-permute-done((bf16[192,1792]{1,0:T(8,128)(2,1)S(1)}, bf16[192,1792]{1,0:T(8,128)(2,1)}, u32[]{:S(2)}, u32[]{:S(2)}) %collective-permute-start.36) | collective-permute-done | bytes 688160 | tf_op jit(solution)/shard_map/ppermute | solution.py:38
  486.4 11.4 %collective-permute-done.45 = f32[1,768]{1,0:T(1,128)S(1)} collective-permute-done((f32[1,768]{1,0:T(1,128)S(1)}, f32[1,768]{1,0:T(1,128)S(1)}, u32[]{:S(2)}, u32[]{:S(2)}) %collective-permute-start.45) | collective-permute-done | bytes 3104 | tf_op jit(solution)/shard_map/ppermute | solution.py:38
  507.8 5.8 %update_inner.1 = (f32[96,2,1536]{2,1,0:T(2,128)}, f32[96,2,1536]{2,1,0:T(2,128)}, f32[96,2,1536]{2,1,0:T(2,128)}, f32[96,2,1536]{2,1,0:T(2,128)}) custom-call(f32[96,1536]{1,0:T(8,128)} %bitcast_add_fusion.9.refs_0_, f32[96,1792]{1,0:T(8,128)} %copy-done.33, f32[96,2,1536]{2,1,0:T(2,128)} %refs_2_.1, f32[96,2,1536]{2,1,0:T(2,128)} %refs_3_.1, ...), custom_call_target="tpu_custom_call" | custom-call | tf_op jit(solution)/shard_map/update_inner/pallas_call | solution.py:226
  (504 shorter events, 236.1 us)
Async XLA Ops:
  9.0 18.0 %collective-permute-start = (bf16[96,1792]{1,0:T(8,128)(2,1)S(1)}, bf16[96,1792]{1,0:T(8,128)(2,1)}, u32[]{:S(2)}, u32[]{:S(2)}) collective-permute-start(bf16[96,1792]{1,0:T(8,128)(2,1)S(1)} %fusion.22), channel_id=1, source_target_pairs={{0,16},{2,18},{4,20},{6,22},{8,24},{10,26},{12,28},{14,30},{16,0},... | collective-permute-start | bytes 1032200 | tf_op jit(solution)/shard_map/ppermute | solution.py:38
  11.6 38.1 %collective-permute-start.10 = (bf16[512,768]{1,0:T(8,128)(2,1)S(1)}, bf16[512,768]{1,0:T(8,128)(2,1)}, u32[]{:S(2)}, u32[]{:S(2)}) collective-permute-start(bf16[512,768]{1,0:T(8,128)(2,1)S(1)} %copy-done.36), channel_id=1, source_target_pairs={{0,1},{1,0},{2,3},{3,2},{4,5},{5,4},{6,7},{7,6},{8,9},{9,8},{10,11... | collective-permute-start | bytes 2359304 | tf_op jit(solution)/shard_map/ppermute | solution.py:38
  53.0 27.4 %collective-permute-start.4 = (bf16[96,3072]{1,0:T(8,128)(2,1)}, bf16[96,3072]{1,0:T(8,128)(2,1)}, u32[]{:S(2)}, u32[]{:S(2)}) collective-permute-start(bf16[96,3072]{1,0:T(8,128)(2,1)} %pad_maximum_fusion.17), channel_id=1, source_target_pairs={{0,16},{2,18},{4,20},{6,22},{8,24},{10,26},{12,28},{14,30},{16,0},... | collective-permute-start | bytes 1769480 | tf_op jit(solution)/shard_map/ppermute | solution.py:38
  65.9 29.5 %collective-permute-start.9 = (bf16[768,896]{1,0:T(8,128)(2,1)}, bf16[768,896]{1,0:T(8,128)(2,1)}, u32[]{:S(2)}, u32[]{:S(2)}) collective-permute-start(bf16[768,896]{1,0:T(8,128)(2,1)} %bitcast.18), channel_id=1, source_target_pairs={{0,4},{2,6},{4,0},{6,2},{8,12},{10,14},{12,8},{14,10},{16,20},{18,... | collective-permute-start | bytes 4128776 | tf_op jit(solution)/shard_map/ppermute | solution.py:38
  66.6 29.2 %collective-permute-start.8 = (bf16[768,896]{1,0:T(8,128)(2,1)S(1)}, bf16[768,896]{1,0:T(8,128)(2,1)}, u32[]{:S(2)}, u32[]{:S(2)}) collective-permute-start(bf16[768,896]{1,0:T(8,128)(2,1)S(1)} %bitcast.284), channel_id=1, source_target_pairs={{0,2},{2,0},{4,6},{6,4},{8,10},{10,8},{12,14},{14,12},{16,18},{18,... | collective-permute-start | bytes 4128776 | tf_op jit(solution)/shard_map/ppermute | solution.py:38
  81.9 27.1 %collective-permute-start.7 = (bf16[192,3072]{1,0:T(8,128)(2,1)S(1)}, bf16[192,3072]{1,0:T(8,128)(2,1)S(1)}, u32[]{:S(2)}, u32[]{:S(2)}) collective-permute-start(bf16[192,3072]{1,0:T(8,128)(2,1)S(1)} %bitcast.295), channel_id=1, source_target_pairs={{0,8},{2,10},{4,12},{6,14},{8,0},{10,2},{12,4},{14,6},{16,24},{18,... | collective-permute-start | bytes 3538952 | tf_op jit(solution)/shard_map/ppermute | solution.py:38
  111.5 29.5 %collective-permute-start.12 = (bf16[384,1536]{1,0:T(8,128)(2,1)}, bf16[384,1536]{1,0:T(8,128)(2,1)}, u32[]{:S(2)}, u32[]{:S(2)}) collective-permute-start(bf16[384,1536]{1,0:T(8,128)(2,1)} %get-tuple-element.447), channel_id=1, source_target_pairs={{0,4},{2,6},{4,0},{6,2},{8,12},{10,14},{12,8},{14,10},{16,20},{18,... | collective-permute-start | bytes 3538952 | tf_op jit(solution)/shard_map/ppermute | solution.py:38
  113.3 27.8 %collective-permute-start.13 = (bf16[384,1536]{1,0:T(8,128)(2,1)}, bf16[384,1536]{1,0:T(8,128)(2,1)}, u32[]{:S(2)}, u32[]{:S(2)}) collective-permute-start(bf16[384,1536]{1,0:T(8,128)(2,1)} %get-tuple-element.446), channel_id=1, source_target_pairs={{0,2},{2,0},{4,6},{6,4},{8,10},{10,8},{12,14},{14,12},{16,18},{18,... | collective-permute-start | bytes 3538952 | tf_op jit(solution)/shard_map/ppermute | solution.py:38
  127.8 37.6 %all-to-all-start = ((f32[16,8,1664]{2,1,0:T(8,128)}), f32[16,8,1664]{2,1,0:T(8,128)}, u32[]{:S(2)}, u32[]{:S(2)}) async-start(f32[16,8,1664]{2,1,0:T(8,128)} %pad_maximum_fusion.15), calls=%async_computation | async-start | bytes 1703936 | tf_op jit(solution)/shard_map/all_to_all | solution.py:195
  146.7 64.6 %collective-permute-start.15 = (bf16[768,1536]{1,0:T(8,128)(2,1)}, bf16[768,1536]{1,0:T(8,128)(2,1)}, u32[]{:S(2)}, u32[]{:S(2)}) collective-permute-start(bf16[768,1536]{1,0:T(8,128)(2,1)} %bitcast.56), channel_id=1, source_target_pairs={{0,4},{2,6},{4,0},{6,2},{8,12},{10,14},{12,8},{14,10},{16,20},{18,... | collective-permute-start | bytes 7077896 | tf_op jit(solution)/shard_map/ppermute | solution.py:38
  152.8 64.5 %collective-permute-start.14 = (bf16[768,1536]{1,0:T(8,128)(2,1)}, bf16[768,1536]{1,0:T(8,128)(2,1)}, u32[]{:S(2)}, u32[]{:S(2)}) collective-permute-start(bf16[768,1536]{1,0:T(8,128)(2,1)} %bitcast.51), channel_id=1, source_target_pairs={{0,2},{2,0},{4,6},{6,4},{8,10},{10,8},{12,14},{14,12},{16,18},{18,... | collective-permute-start | bytes 7077896 | tf_op jit(solution)/shard_map/ppermute | solution.py:38
  169.3 41.9 %all-to-all-start.1 = ((f32[16,8,1536]{2,1,0:T(8,128)}), f32[16,8,1536]{2,1,0:T(8,128)}, u32[]{:S(2)}, u32[]{:S(2)}) async-start(f32[16,8,1536]{2,1,0:T(8,128)} %walk.2), calls=%async_computation.1 | async-start | bytes 1572864 | tf_op jit(solution)/shard_map/all_to_all | solution.py:206
  241.4 40.2 %all-to-all-start.2 = ((f32[16,8,1536]{2,1,0:T(8,128)}), f32[16,8,1536]{2,1,0:T(8,128)}, u32[]{:S(2)}, u32[]{:S(2)}) async-start(f32[16,8,1536]{2,1,0:T(8,128)} %bitcast.334), calls=%async_computation.2 | async-start | bytes 1572864 | tf_op jit(solution)/shard_map/all_to_all | solution.py:195
  283.9 26.8 %all-to-all-start.3 = ((f32[16,8,1536]{2,1,0:T(8,128)}), f32[16,8,1536]{2,1,0:T(8,128)}, u32[]{:S(2)}, u32[]{:S(2)}) async-start(f32[16,8,1536]{2,1,0:T(8,128)} %walk.3), calls=%async_computation.3 | async-start | bytes 1572864 | tf_op jit(solution)/shard_map/all_to_all | solution.py:206
  294.3 40.3 %collective-permute-start.19 = (bf16[768,768]{1,0:T(8,128)(2,1)}, bf16[768,768]{1,0:T(8,128)(2,1)}, u32[]{:S(2)}, u32[]{:S(2)}) collective-permute-start(bf16[768,768]{1,0:T(8,128)(2,1)} %convolution_convert_fusion.4), channel_id=1, source_target_pairs={{0,2},{2,0},{4,6},{6,4},{8,10},{10,8},{12,14},{14,12},{16,18},{18,... | collective-permute-start | bytes 3538952 | tf_op jit(solution)/shard_map/ppermute | solution.py:38
  296.1 38.4 %collective-permute-start.18 = (bf16[768,768]{1,0:T(8,128)(2,1)}, bf16[768,768]{1,0:T(8,128)(2,1)}, u32[]{:S(2)}, u32[]{:S(2)}) collective-permute-start(bf16[768,768]{1,0:T(8,128)(2,1)} %convolution_convert_fusion.5), channel_id=1, source_target_pairs={{0,4},{2,6},{4,0},{6,2},{8,12},{10,14},{12,8},{14,10},{16,20},{18,... | collective-permute-start | bytes 3538952 | tf_op jit(solution)/shard_map/ppermute | solution.py:38
  301.0 52.6 %collective-permute-start.21 = (bf16[768,768]{1,0:T(8,128)(2,1)}, bf16[768,768]{1,0:T(8,128)(2,1)}, u32[]{:S(2)}, u32[]{:S(2)}) collective-permute-start(bf16[768,768]{1,0:T(8,128)(2,1)} %convolution_convert_fusion.2), channel_id=1, source_target_pairs={{0,2},{2,0},{4,6},{6,4},{8,10},{10,8},{12,14},{14,12},{16,18},{18,... | collective-permute-start | bytes 3538952 | tf_op jit(solution)/shard_map/ppermute | solution.py:38
  303.4 50.3 %collective-permute-start.20 = (bf16[768,768]{1,0:T(8,128)(2,1)}, bf16[768,768]{1,0:T(8,128)(2,1)}, u32[]{:S(2)}, u32[]{:S(2)}) collective-permute-start(bf16[768,768]{1,0:T(8,128)(2,1)} %convolution_convert_fusion.3), channel_id=1, source_target_pairs={{0,4},{2,6},{4,0},{6,2},{8,12},{10,14},{12,8},{14,10},{16,20},{18,... | collective-permute-start | bytes 3538952 | tf_op jit(solution)/shard_map/ppermute | solution.py:38
  333.1 42.5 %collective-permute-start.22 = (f32[3,1664]{1,0:T(4,128)}, f32[3,1664]{1,0:T(4,128)}, u32[]{:S(2)}, u32[]{:S(2)}) collective-permute-start(f32[3,1664]{1,0:T(4,128)} %pad_add_fusion.3), channel_id=1, source_target_pairs={{2,0},{4,2},{6,4},{8,6},{10,8},{12,10},{14,12},{16,14},{18,16},{20... | collective-permute-start | bytes 59912 | tf_op jit(solution)/shard_map/ppermute | solution.py:33
  364.4 29.1 %collective-permute-start.24 = (bf16[384,1536]{1,0:T(8,128)(2,1)}, bf16[384,1536]{1,0:T(8,128)(2,1)}, u32[]{:S(2)}, u32[]{:S(2)}) collective-permute-start(bf16[384,1536]{1,0:T(8,128)(2,1)} %bitcast.79), channel_id=1, source_target_pairs={{0,4},{2,6},{4,0},{6,2},{8,12},{10,14},{12,8},{14,10},{16,20},{18,... | collective-permute-start | bytes 3538952 | tf_op jit(solution)/shard_map/ppermute | solution.py:38
  366.0 27.6 %collective-permute-start.23 = (bf16[384,1536]{1,0:T(8,128)(2,1)}, bf16[384,1536]{1,0:T(8,128)(2,1)}, u32[]{:S(2)}, u32[]{:S(2)}) collective-permute-start(bf16[384,1536]{1,0:T(8,128)(2,1)} %bitcast.77), channel_id=1, source_target_pairs={{0,2},{2,0},{4,6},{6,4},{8,10},{10,8},{12,14},{14,12},{16,18},{18,... | collective-permute-start | bytes 3538952 | tf_op jit(solution)/shard_map/ppermute | solution.py:38
  391.6 34.5 %collective-permute-start.27 = (bf16[768,896]{1,0:T(8,128)(2,1)S(1)}, bf16[768,896]{1,0:T(8,128)(2,1)S(1)}, u32[]{:S(2)}, u32[]{:S(2)}) collective-permute-start(bf16[768,896]{1,0:T(8,128)(2,1)S(1)} %convolution_convert_fusion), channel_id=1, source_target_pairs={{0,4},{2,6},{4,0},{6,2},{8,12},{10,14},{12,8},{14,10},{16,20},{18,... | collective-permute-start | bytes 4128776 | tf_op jit(solution)/shard_map/ppermute | solution.py:38
  392.0 34.1 %collective-permute-start.26 = (bf16[768,896]{1,0:T(8,128)(2,1)S(1)}, bf16[768,896]{1,0:T(8,128)(2,1)S(1)}, u32[]{:S(2)}, u32[]{:S(2)}) collective-permute-start(bf16[768,896]{1,0:T(8,128)(2,1)S(1)} %convolution_convert_fusion.1), channel_id=1, source_target_pairs={{0,2},{2,0},{4,6},{6,4},{8,10},{10,8},{12,14},{14,12},{16,18},{18,... | collective-permute-start | bytes 4128776 | tf_op jit(solution)/shard_map/ppermute | solution.py:38
  397.4 27.4 %collective-permute-start.29 = (bf16[192,1536]{1,0:T(8,128)(2,1)S(1)}, bf16[192,1536]{1,0:T(8,128)(2,1)S(1)}, u32[]{:S(2)}, u32[]{:S(2)}) collective-permute-start(bf16[192,1536]{1,0:T(8,128)(2,1)S(1)} %bitcast.341), channel_id=1, source_target_pairs={{0,8},{2,10},{4,12},{6,14},{8,0},{10,2},{12,4},{14,6},{16,24},{18,... | collective-permute-start | bytes 1769480 | tf_op jit(solution)/shard_map/ppermute | solution.py:38
  399.7 25.1 %collective-permute-start.28 = (bf16[192,1536]{1,0:T(8,128)(2,1)S(1)}, bf16[192,1536]{1,0:T(8,128)(2,1)S(1)}, u32[]{:S(2)}, u32[]{:S(2)}) collective-permute-start(bf16[192,1536]{1,0:T(8,128)(2,1)S(1)} %bitcast.342), channel_id=1, source_target_pairs={{0,8},{2,10},{4,12},{6,14},{8,0},{10,2},{12,4},{14,6},{16,24},{18,... | collective-permute-start | bytes 1769480 | tf_op jit(solution)/shard_map/ppermute | solution.py:38
  421.8 25.9 %collective-permute-start.25 = (f32[512,768]{1,0:T(8,128)S(1)}, f32[512,768]{1,0:T(8,128)S(1)}, u32[]{:S(2)}, u32[]{:S(2)}) collective-permute-start(f32[512,768]{1,0:T(8,128)S(1)} %get-tuple-element.438), channel_id=1, source_target_pairs={{0,1},{1,0},{2,3},{3,2},{4,5},{5,4},{6,7},{7,6},{8,9},{9,8},{10,11... | collective-permute-start | bytes 4718600 | tf_op jit(solution)/shard_map/ppermute | solution.py:38
  426.5 17.9 %collective-permute-start.34 = (bf16[384,896]{1,0:T(8,128)(2,1)S(1)}, bf16[384,896]{1,0:T(8,128)(2,1)S(1)}, u32[]{:S(2)}, u32[]{:S(2)}) collective-permute-start(bf16[384,896]{1,0:T(8,128)(2,1)S(1)} %bitcast.337), channel_id=1, source_target_pairs={{0,4},{2,6},{4,0},{6,2},{8,12},{10,14},{12,8},{14,10},{16,20},{18,... | collective-permute-start | bytes 2064392 | tf_op jit(solution)/shard_map/ppermute | solution.py:38
  430.6 50.9 %collective-permute-start.33 = (bf16[96,1536]{1,0:T(8,128)(2,1)S(1)}, bf16[96,1536]{1,0:T(8,128)(2,1)}, u32[]{:S(2)}, u32[]{:S(2)}) collective-permute-start(bf16[96,1536]{1,0:T(8,128)(2,1)S(1)} %fusion.25), channel_id=1, source_target_pairs={{0,16},{2,18},{4,20},{6,22},{8,24},{10,26},{12,28},{14,30},{16,0},... | collective-permute-start | bytes 884744 | tf_op jit(solution)/shard_map/ppermute | solution.py:38
  433.5 48.0 %collective-permute-start.32 = (bf16[96,1536]{1,0:T(8,128)(2,1)}, bf16[96,1536]{1,0:T(8,128)(2,1)}, u32[]{:S(2)}, u32[]{:S(2)}) collective-permute-start(bf16[96,1536]{1,0:T(8,128)(2,1)} %fusion.24), channel_id=1, source_target_pairs={{0,16},{2,18},{4,20},{6,22},{8,24},{10,26},{12,28},{14,30},{16,0},... | collective-permute-start | bytes 884744 | tf_op jit(solution)/shard_map/ppermute | solution.py:38
  457.1 18.2 %collective-permute-start.36 = (bf16[192,1792]{1,0:T(8,128)(2,1)S(1)}, bf16[192,1792]{1,0:T(8,128)(2,1)}, u32[]{:S(2)}, u32[]{:S(2)}) collective-permute-start(bf16[192,1792]{1,0:T(8,128)(2,1)S(1)} %bitcast.336), channel_id=1, source_target_pairs={{0,8},{2,10},{4,12},{6,14},{8,0},{10,2},{12,4},{14,6},{16,24},{18,... | collective-permute-start | bytes 2064392 | tf_op jit(solution)/shard_map/ppermute | solution.py:38
  462.8 37.6 %collective-permute-start.30 = (f32[512,768]{1,0:T(8,128)}, f32[512,768]{1,0:T(8,128)}, u32[]{:S(2)}, u32[]{:S(2)}) collective-permute-start(f32[512,768]{1,0:T(8,128)} %slice_select_fusion.1), channel_id=1, source_target_pairs={{0,1},{1,0},{2,3},{3,2},{4,5},{5,4},{6,7},{7,6},{8,9},{9,8},{10,11... | collective-permute-start | bytes 4718600 | tf_op jit(solution)/shard_map/ppermute | solution.py:38
  480.1 24.0 %collective-permute-start.37 = (bf16[96,1792]{1,0:T(8,128)(2,1)S(1)}, bf16[96,1792]{1,0:T(8,128)(2,1)S(1)}, u32[]{:S(2)}, u32[]{:S(2)}) collective-permute-start(bf16[96,1792]{1,0:T(8,128)(2,1)S(1)} %fusion.23), channel_id=1, source_target_pairs={{0,16},{2,18},{4,20},{6,22},{8,24},{10,26},{12,28},{14,30},{16,0},... | collective-permute-start | bytes 1032200 | tf_op jit(solution)/shard_map/ppermute | solution.py:38
  (123 other events, 1101.1 us)
where the time goes:
time: 519 us; the launch traced here: 514 us
  waiting for transfers between devices  137 us (26%)
  other arithmetic  97.6 us (19%)
  starting transfers between devices  89.5 us (17%)
  Pallas kernels  69.3 us (13%)
  matrix products  64.6 us (12%)
  local copies, waits for them, and re-layouts  53.3 us (10%)
    ppermute x45, waiting for transfers between devices, swap(): return lax.ppermute(array, axis, [(i, i ^ mask) for i in range(count)])  120 us
    ppermute x45, starting transfers between devices, swap(): return lax.ppermute(array, axis, [(i, i ^ mask) for i in range(count)])  48.4 us
    dot_general x10, matrix products, token_product(): lax.dot_general(left, right, (((0,), (0,)), ((), ())), preferred_element_...  21.2 us
    unnamed x221, local copies, waits for them, and re-layouts  20.7 us
    pallas_call x1, Pallas kernels, span_backs(): pl.pallas_call(span_back_kernel, grid=(rows // CH, width // wide), in_spe...  19.2 us
    all_to_all x2, starting transfers between devices, walked_in(): back = lax.all_to_all(walked, axis, 0, 0)  18.4 us
    all_to_all x2, starting transfers between devices, parts_out(): return lax.all_to_all(pieces, axis, 0, 0)  16.3 us
    all_to_all x2, waiting for transfers between devices, walked_in(): back = lax.all_to_all(walked, axis, 0, 0)  16.2 us
  transfers between devices with their start and end apart: 51, of which 20 were waited for; matrix products, arithmetic and copies ran while one was open for 37% of the time, Pallas kernels for 9%

commit v1 on v0

--- a/solution.py
+++ b/solution.py
@@ -662,7 +662,7 @@
     orders = bit_orders(SEQ)
     far = orders[0][:1:-1]
     near = [order[1::-1] for order in orders]
-    begun = gather_rows(shard_a, SEQ, far[:1])
+    begun = gather_rows(shard_a, SEQ, far[:1], ())
     other = swap(begun, SEQ, 1 << far[1]) if len(far) > 1 else begun
     edge_own = shifted(tokens[local_rows - 8 :], SEQ, 1)
     tokens_ext = jnp.concatenate([edge_own, tokens], 0)
@@ -685,10 +685,11 @@
     other_a = [swap(held_a[k], SEQ, 1 << near[k][0]) for k in range(2)]
     held_bc = after(held_bc, begun)
     other_bc = swap(held_bc, SEQ, 1 << far[0])
-    grads_in = side_by_side(cotangent, swap(cotangent, HEAD, 1), upper)
+    grads_got = swap(cotangent, HEAD, 1)
     held_a = [assemble(held_a[k], other_a[k], SEQ, near[k][0], far) for k in range(2)]
     other_a = [swap(held_a[k], SEQ, 1 << near[k][1]) for k in range(2)]
-    normed_ext = after(normed_ext, held_a)
+    normed_ext, grads_got = after((normed_ext, grads_got), held_a)
+    grads_in = side_by_side(cotangent, grads_got, upper)
     ext_sides = [
         [pick_columns(normed_ext, SEQ, order[0], other) for other in (False, True)]
         for order in orders
@@ -879,23 +880,11 @@
     d_conv = jnp.concatenate([d_values, group_share], 1) * silu_slope(conv_out)
     d_taps, ext_grad = conv_backward(extended, tap_rows, masks, d_conv, KC)
     from_next = after(from_next, sent_bc)
-    rest = orders[0][2:]
     d_conv_in = ext_grad[edge_count:] + jnp.pad(from_next, ((local_rows - edge_count, 0), (0, 0)))
     grads_a = jnp.concatenate(
         [d_conv_in.astype(bf16), jnp.pad(d_step_low, ((0, 0), (0, pad_heads)))], 1
     )
-    parts_a = [grads_a[:, :cut], grads_a[:, cut:]]
-    sent_a = [token_product(normed_sides[k][1], parts_a[k]).astype(bf16) for k in range(2)]
-    got_a = [swap(sent_a[k], SEQ, 1 << orders[k][0]) for k in range(2)]
-    parts_a, held_a, other_a, held_bc, other_bc, got_bc = after(
-        (parts_a, held_a, other_a, held_bc, other_bc, got_bc), sent_a
-    )
-    full_a = [
-        assemble(held_a[k], other_a[k], SEQ, near[k][1], far + near[k][:1]) for k in range(2)
-    ]
-    full_b, full_c = [
-        assemble(held_bc[k], other_bc[k], SEQ, near[k][1], far + near[k][:1]) for k in range(2)
-    ]
+    rest = orders[0][2:]
     heads_flat = jnp.concatenate([d_bias, d_alog, d_skip])
     small = jnp.concatenate(
         [
@@ -905,23 +894,36 @@
         ],
         0,
     )
-    small = butterfly_sum(after(small, sent_a), SEQ, orders[0][2:])
-    d_normed_own, d_normed_other = split_features(
+    small = butterfly_sum(small, SEQ, rest)
+    parts_a = [grads_a[:, :cut], grads_a[:, cut:]]
+    sent_a = [token_product(normed_sides[k][1], parts_a[k]).astype(bf16) for k in range(2)]
+    got_a = [swap(sent_a[k], SEQ, 1 << orders[k][0]) for k in range(2)]
+    parts_a, held_a, other_a, held_bc, other_bc = after(
+        (parts_a, held_a, other_a, held_bc, other_bc), sent_a
+    )
+    kept_bc, got_bc = after((kept_bc, got_bc), sent_a)
+    held_bc_grad = [k + g.astype(f32) for k, g in zip(kept_bc, got_bc)]
+    kept_bc, sent_bc = zip(*[sides_of(h, SEQ, rest[0], rest) for h in held_bc_grad])
+    got_bc = [swap(sent, SEQ, 1 << rest[0]) for sent in sent_bc]
+    held_a = after(held_a, sent_bc)
+    full_a = [
+        assemble(held_a[k], other_a[k], SEQ, near[k][1], far + near[k][:1]) for k in range(2)
+    ]
+    full_b = assemble(held_bc[0], other_bc[0], SEQ, near[0][1], far + near[0][:1])
+    d_normed_part = (
         back_product(d_gate, full_b)
         + back_product(parts_a[0], full_a[0])
         + back_product(parts_a[1], full_a[1])
     )
-    d_normed_got = swap(d_normed_other, HEAD, 1)
-    held_bc_grad = [k + g.astype(f32) for k, g in zip(kept_bc, got_bc)]
-    kept_bc, sent_bc = zip(*[sides_of(h, SEQ, rest[0], rest) for h in held_bc_grad])
-    got_bc = [swap(sent, SEQ, 1 << rest[0]) for sent in sent_bc]
-    got_bc = after(got_bc, d_normed_other)
+    got_bc = after(got_bc, d_normed_part)
     held_bc_grad = [k + g.astype(f32) for k, g in zip(kept_bc, got_bc)]
     if len(rest) > 1:
         kept_bc, sent_bc = zip(*[sides_of(h, SEQ, rest[1], rest[1:]) for h in held_bc_grad])
         got_bc = [swap(sent, SEQ, 1 << rest[1]) for sent in sent_bc]
+    d_normed_own, d_normed_other = split_features(d_normed_part)
+    d_normed_got = swap(d_normed_other, HEAD, 1)
     kept_a = [token_product(normed_sides[k][0], parts_a[k]) for k in range(2)]
-    kept_a, got_a = after((kept_a, got_a), sent_bc, d_normed_other)
+    kept_a, got_a = after((kept_a, got_a), d_normed_other, sent_bc)
     kept_a, sent_a = zip(
         *[
             sides_of(kept_a[k] + got_a[k].astype(f32), SEQ, orders[k][1], orders[k][1:])
@@ -929,9 +931,10 @@
         ]
     )
     got_a = [swap(sent_a[k], SEQ, 1 << orders[k][1]) for k in range(2)]
-    d_normed_own, d_normed_got, mixed, full_c = after(
-        (d_normed_own, d_normed_got, mixed, full_c), sent_a
-    )
+    d_normed_own, d_normed_got, mixed, held_bc, other_bc = after(
+        (d_normed_own, d_normed_got, mixed, held_bc, other_bc), sent_a
+    )
+    full_c = assemble(held_bc[1], other_bc[1], SEQ, near[1][1], far + near[1][:1])
     d_normed = d_normed_own + d_normed_got
     own_unit = jnp.where(upper, unit_rows[:, share:], unit_rows[:, :share])
     own_gain = jnp.where(upper, prenorm_weight[share:], prenorm_weight[:share])

time: 519 us -> 516 us (level)
  waiting for transfers between devices: 137 us -> 148 us
  starting transfers between devices: 89.5 us -> 81 us
  other arithmetic: 97.6 us -> 91.8 us
    ppermute x45, waiting for transfers between devices: 120 us -> 132 us  [swap(): return lax.ppermute(array, axis, [(i, i ^ mask) for i in range(count)])]
    ppermute x45, starting transfers between devices: 48.4 us -> 40.1 us  [swap(): return lax.ppermute(array, axis, [(i, i ^ mask) for i in range(count)])]
    unnamed x221 -> x219, local copies, waits for them, and re-layouts: 20.7 us -> 17 us
  transfers between devices with their start and end apart: 51 -> 51, of which waited for: 20 -> 22; matrix products, arithmetic and copies ran while one was open for 37% -> 37% of each run, Pallas kernels for 9% -> 9%
where the time goes in v1:
time: 516 us; the launch traced here: 510 us
  waiting for transfers between devices  148 us (29%)
  other arithmetic  91.8 us (18%)
  starting transfers between devices  81 us (16%)
  Pallas kernels  69.3 us (13%)
  matrix products  62.8 us (12%)
  local copies, waits for them, and re-layouts  54.1 us (10%)
    ppermute x45, waiting for transfers between devices, swap(): return lax.ppermute(array, axis, [(i, i ^ mask) for i in range(count)])  132 us
    ppermute x45, starting transfers between devices, swap(): return lax.ppermute(array, axis, [(i, i ^ mask) for i in range(count)])  40.1 us
    dot_general x10, matrix products, token_product(): lax.dot_general(left, right, (((0,), (0,)), ((), ())), preferred_element_...  21 us
    pallas_call x1, Pallas kernels, span_backs(): pl.pallas_call(span_back_kernel, grid=(rows // CH, width // wide), in_spe...  19.1 us
    all_to_all x2, starting transfers between devices, walked_in(): back = lax.all_to_all(walked, axis, 0, 0)  18.3 us
    unnamed x219, local copies, waits for them, and re-layouts  17 us
    all_to_all x2, waiting for transfers between devices, walked_in(): back = lax.all_to_all(walked, axis, 0, 0)  16.3 us
    all_to_all x2, starting transfers between devices, parts_out(): return lax.all_to_all(pieces, axis, 0, 0)  16.3 us
  transfers between devices with their start and end apart: 51, of which 22 were waited for; matrix products, arithmetic and copies ran while one was open for 37% of the time, Pallas kernels for 9%

profile of v1, /device:TPU:0, one launch (start us, length us, event | category | flops | bytes accessed | tf_op | source)
XLA Modules:
  0.0 510.3 jit_solution(5467252510238932853)
XLA Ops:
  1.5 4.9 collective-permute-start.2
  15.5 11.3 %collective-permute-done = bf16[96,1792]{1,0:T(8,128)(2,1)S(1)} collective-permute-done((bf16[96,1792]{1,0:T(8,128)(2,1)}, bf16[96,1792]{1,0:T(8,128)(2,1)S(1)}, u32[]{:S(2)}, u32[]{:S(2)}) %collective-permute-start) | collective-permute-done | bytes 344096 | tf_op jit(solution)/shard_map/ppermute | solution.py:38
  30.1 13.4 %collective-permute-done.1 = bf16[192,1792]{1,0:T(8,128)(2,1)S(1)} collective-permute-done((bf16[192,1792]{1,0:T(8,128)(2,1)S(1)}, bf16[192,1792]{1,0:T(8,128)(2,1)S(1)}, u32[]{:S(2)}, u32[]{:S(2)}) %collective-permute-start.1) | collective-permute-done | bytes 688160 | tf_op jit(solution)/shard_map/ppermute | solution.py:38
  50.9 8.8 %collective-permute-done.5 = bf16[384,896]{1,0:T(8,128)(2,1)S(1)} collective-permute-done((bf16[384,896]{1,0:T(8,128)(2,1)S(1)}, bf16[384,896]{1,0:T(8,128)(2,1)S(1)}, u32[]{:S(2)}, u32[]{:S(2)}) %collective-permute-start.5) | collective-permute-done | bytes 688160 | tf_op jit(solution)/shard_map/ppermute | solution.py:38
  72.0 4.5 collective-permute-done.4
  85.3 8.1 %collective-permute-done.9 = bf16[768,896]{1,0:T(8,128)(2,1)} collective-permute-done((bf16[768,896]{1,0:T(8,128)(2,1)}, bf16[768,896]{1,0:T(8,128)(2,1)}, u32[]{:S(2)}, u32[]{:S(2)}) %collective-permute-start.9) | collective-permute-done | bytes 1376288 | tf_op jit(solution)/shard_map/ppermute | solution.py:38
  99.2 5.8 %collective-permute-done.7 = bf16[192,3072]{1,0:T(8,128)(2,1)S(1)} collective-permute-done((bf16[192,3072]{1,0:T(8,128)(2,1)S(1)}, bf16[192,3072]{1,0:T(8,128)(2,1)S(1)}, u32[]{:S(2)}, u32[]{:S(2)}) %collective-permute-start.7) | collective-permute-done | bytes 1179680 | tf_op jit(solution)/shard_map/ppermute | solution.py:38
  110.6 4.2 multiply_convert_fusion
  123.2 7.3 %all-to-all-start = ((f32[16,8,1664]{2,1,0:T(8,128)}), f32[16,8,1664]{2,1,0:T(8,128)}, u32[]{:S(2)}, u32[]{:S(2)}) async-start(f32[16,8,1664]{2,1,0:T(8,128)} %pad_maximum_fusion.15), calls=%async_computation | async-start | bytes 1703936 | tf_op jit(solution)/shard_map/all_to_all | solution.py:195
  130.5 6.6 %collective-permute-done.12 = bf16[384,1536]{1,0:T(8,128)(2,1)} collective-permute-done((bf16[384,1536]{1,0:T(8,128)(2,1)}, bf16[384,1536]{1,0:T(8,128)(2,1)}, u32[]{:S(2)}, u32[]{:S(2)}) %collective-permute-start.12) | collective-permute-done | bytes 1179680 | tf_op jit(solution)/shard_map/ppermute | solution.py:38
  137.1 4.0 broadcast_select_fusion.9
  152.9 8.5 %span_outputs.1.refs_0_.all_refs_0_ = f32[512,1536]{1,0:T(8,128)} custom-call(f32[24,512]{1,0:T(8,128)} %bitcast.340, f32[24,512]{1,0:T(8,128)} %copy.186.step_ref, s32[1,512]{1,0:T(1,128)} %bitcast.342, s32[512,1]{1,0:T(8,128)} %copy.187.seg_col_ref, bf16[512,128]{1,0:T(8,128)(2,1)} %copy-done.32, ...), custom_call_target="tpu_custom_call" | custom-call | tf_op jit(solution)/shard_map/span_outputs/pallas_call | solution.py:500
  165.2 11.2 %all-to-all-start.1 = ((f32[16,8,1536]{2,1,0:T(8,128)}), f32[16,8,1536]{2,1,0:T(8,128)}, u32[]{:S(2)}, u32[]{:S(2)}) async-start(f32[16,8,1536]{2,1,0:T(8,128)} %walk.2), calls=%async_computation.1 | async-start | bytes 1572864 | tf_op jit(solution)/shard_map/all_to_all | solution.py:206
  181.3 4.8 fusion.68
  186.1 4.7 fusion.67
  190.8 16.3 %all-to-all-done.1 = f32[16,8,1536]{2,1,0:T(8,128)} async-done(((f32[16,8,1536]{2,1,0:T(8,128)}), f32[16,8,1536]{2,1,0:T(8,128)}, u32[]{:S(2)}, u32[]{:S(2)}) %all-to-all-start.1) | async-done | bytes 786464 | tf_op jit(solution)/shard_map/all_to_all | solution.py:206
  207.2 6.1 %convolution_add_fusion.refs_2_.all_refs_2_ = f32[512,1536]{1,0:T(8,128)} fusion(f32[512,1536]{1,0:T(8,128)} %fusion.68, bf16[512,768]{0,1:T(8,128)(2,1)} %bitcast.313, bf16[768,1536]{1,0:T(8,128)(2,1)} %collective-permute-done.15), kind=kOutput, calls=%fused_computation.24 | convolution fusion | flops 1208745984 | bytes 9437184 | tf_op jit(solution)/shard_map/dot_general | solution.py:790
  213.3 4.8 convolution_add_fusion.1.refs_1_.all_refs_1_
  218.2 6.5 %row_sums.1.all_refs_9_ = f32[512,128]{1,0:T(8,128)} custom-call(f32[512,1536]{1,0:T(8,128)} %span_outputs.1.refs_0_.all_refs_0_, f32[512,1536]{1,0:T(8,128)} %convolution_add_fusion.1.refs_1_.all_refs_1_, f32[512,1536]{1,0:T(8,128)} %convolution_add_fusion.refs_2_.all_refs_2_, bf16[512,128]{1,0:T(8,128)(2,1)} %get-tuple-element.472.c_ref.refs_3_.all_refs_3_, ...), custom_call_target="tpu_custom_call" | custom-call | tf_op jit(solution)/shard_map/row_sums/pallas_call | solution.py:311
  226.5 10.8 %middle.1 = (bf16[512,1536]{1,0:T(8,128)(2,1)}, bf16[512,1536]{1,0:T(8,128)(2,1)}, bf16[512,1536]{1,0:T(8,128)(2,1)}, f32[1,1536]{1,0:T(1,128)}, f32[128,1536]{1,0:T(8,128)}, /*index=5*/f32[128,1536]{1,0:T(8,128)}) custom-call(f32[512,1536]{1,0:T(8,128)} %span_outputs.1.refs_0_.all_refs_0_, f32[512,1536]{1,0:T(8,128)} %convolution_add_fusion.1.refs_1_.all_refs_1_, ...), custom_call_target="tpu_custom_call" | custom-call | tf_op jit(solution)/shard_map/middle/pallas_call | solution.py:357
  237.3 9.0 %all-to-all-start.2 = ((f32[16,8,1536]{2,1,0:T(8,128)}), f32[16,8,1536]{2,1,0:T(8,128)}, u32[]{:S(2)}, u32[]{:S(2)}) async-start(f32[16,8,1536]{2,1,0:T(8,128)} %bitcast.332), calls=%async_computation.2 | async-start | bytes 1572864 | tf_op jit(solution)/shard_map/all_to_all | solution.py:195
  258.8 19.1 %span_backs.1 = (f32[512,1536]{1,0:T(8,128)}, f32[24,512]{1,0:T(8,128)}, f32[24,512]{1,0:T(8,128)}, f32[512,128]{1,0:T(8,128)}, f32[512,128]{1,0:T(8,128)}) custom-call(f32[24,512]{1,0:T(8,128)} %bitcast.341, f32[24,512]{1,0:T(8,128)} %copy.186.step_ref, s32[1,512]{1,0:T(1,128)} %bitcast.343, s32[512,1]{1,0:T(8,128)} %copy.187.seg_col_ref, ...), custom_call_target="tpu_custom_call" | custom-call | tf_op jit(solution)/shard_map/span_backs/pallas_call | solution.py:575
  280.1 7.1 %all-to-all-start.3 = ((f32[16,8,1536]{2,1,0:T(8,128)}), f32[16,8,1536]{2,1,0:T(8,128)}, u32[]{:S(2)}, u32[]{:S(2)}) async-start(f32[16,8,1536]{2,1,0:T(8,128)} %walk.3), calls=%async_computation.3 | async-start | bytes 1572864 | tf_op jit(solution)/shard_map/all_to_all | solution.py:206
  307.4 14.3 %late.1 = (f32[512,1536]{1,0:T(8,128)}, f32[512,128]{1,0:T(8,128)}, f32[512,128]{1,0:T(8,128)}, f32[512,24]{1,0:T(8,128)}, f32[512,24]{1,0:T(8,128)}, /*index=5*/f32[2,8,128]{2,1,0:T(8,128)}) custom-call(bf16[512,1664]{1,0:T(8,128)(2,1)} %copy-done, bf16[512,1536]{1,0:T(8,128)(2,1)} %get-tuple-element.167.g_ref, bf16[512,128]{1,0:T(8,128)(2,1)} %copy-done.32, ...), custom_call_target="tpu_custom_call" | custom-call | tf_op jit(solution)/shard_map/late/pallas_call | solution.py:453
  331.9 17.0 %collective-permute-done.21 = bf16[768,768]{1,0:T(8,128)(2,1)} collective-permute-done((bf16[768,768]{1,0:T(8,128)(2,1)}, bf16[768,768]{1,0:T(8,128)(2,1)}, u32[]{:S(2)}, u32[]{:S(2)}) %collective-permute-start.21) | collective-permute-done | bytes 1179680 | tf_op jit(solution)/shard_map/ppermute | solution.py:38
  362.8 4.9 multiply_reduce_fusion
  406.5 4.8 collective-permute-done.29
  411.3 9.5 %collective-permute-done.28 = bf16[192,1536]{1,0:T(8,128)(2,1)S(1)} collective-permute-done((bf16[192,1536]{1,0:T(8,128)(2,1)S(1)}, bf16[192,1536]{1,0:T(8,128)(2,1)S(1)}, u32[]{:S(2)}, u32[]{:S(2)}) %collective-permute-start.28) | collective-permute-done | bytes 589856 | tf_op jit(solution)/shard_map/ppermute | solution.py:38
  429.8 8.3 %collective-permute-done.34 = bf16[384,896]{1,0:T(8,128)(2,1)S(1)} collective-permute-done((bf16[384,896]{1,0:T(8,128)(2,1)S(1)}, bf16[384,896]{1,0:T(8,128)(2,1)S(1)}, u32[]{:S(2)}, u32[]{:S(2)}) %collective-permute-start.34) | collective-permute-done | bytes 688160 | tf_op jit(solution)/shard_map/ppermute | solution.py:38
  461.8 11.4 %collective-permute-done.36 = bf16[192,1792]{1,0:T(8,128)(2,1)} collective-permute-done((bf16[192,1792]{1,0:T(8,128)(2,1)}, bf16[192,1792]{1,0:T(8,128)(2,1)}, u32[]{:S(2)}, u32[]{:S(2)}) %collective-permute-start.36) | collective-permute-done | bytes 688160 | tf_op jit(solution)/shard_map/ppermute | solution.py:38
  482.2 11.6 %collective-permute-done.45 = f32[1,768]{1,0:T(1,128)S(1)} collective-permute-done((f32[1,768]{1,0:T(1,128)S(1)}, f32[1,768]{1,0:T(1,128)S(1)}, u32[]{:S(2)}, u32[]{:S(2)}) %collective-permute-start.45) | collective-permute-done | bytes 3104 | tf_op jit(solution)/shard_map/ppermute | solution.py:38
  504.1 5.8 %update_inner.1 = (f32[96,2,1536]{2,1,0:T(2,128)}, f32[96,2,1536]{2,1,0:T(2,128)}, f32[96,2,1536]{2,1,0:T(2,128)}, f32[96,2,1536]{2,1,0:T(2,128)}) custom-call(f32[96,1536]{1,0:T(8,128)} %bitcast_add_fusion.7.refs_0_, f32[96,1792]{1,0:T(8,128)} %copy-done.34, f32[96,2,1536]{2,1,0:T(2,128)} %refs_2_.1, f32[96,2,1536]{2,1,0:T(2,128)} %refs_3_.1, ...), custom_call_target="tpu_custom_call" | custom-call | tf_op jit(solution)/shard_map/update_inner/pallas_call | solution.py:226
  (501 shorter events, 231.9 us)
Async XLA Ops:
  8.8 18.0 %collective-permute-start = (bf16[96,1792]{1,0:T(8,128)(2,1)}, bf16[96,1792]{1,0:T(8,128)(2,1)S(1)}, u32[]{:S(2)}, u32[]{:S(2)}) collective-permute-start(bf16[96,1792]{1,0:T(8,128)(2,1)} %fusion.22), channel_id=1, source_target_pairs={{0,16},{2,18},{4,20},{6,22},{8,24},{10,26},{12,28},{14,30},{16,0},... | collective-permute-start | bytes 1032200 | tf_op jit(solution)/shard_map/ppermute | solution.py:38
  11.4 54.5 %collective-permute-start.10 = (bf16[512,768]{1,0:T(8,128)(2,1)}, bf16[512,768]{1,0:T(8,128)(2,1)}, u32[]{:S(2)}, u32[]{:S(2)}) collective-permute-start(bf16[512,768]{1,0:T(8,128)(2,1)} %param.32), channel_id=1, source_target_pairs={{0,1},{1,0},{2,3},{3,2},{4,5},{5,4},{6,7},{7,6},{8,9},{9,8},{10,11... | collective-permute-start | bytes 2359304 | tf_op jit(solution)/shard_map/ppermute | solution.py:38
  27.0 16.5 %collective-permute-start.1 = (bf16[192,1792]{1,0:T(8,128)(2,1)S(1)}, bf16[192,1792]{1,0:T(8,128)(2,1)S(1)}, u32[]{:S(2)}, u32[]{:S(2)}) collective-permute-start(bf16[192,1792]{1,0:T(8,128)(2,1)S(1)} %bitcast.337), channel_id=1, source_target_pairs={{0,8},{2,10},{4,12},{6,14},{8,0},{10,2},{12,4},{14,6},{16,24},{18,... | collective-permute-start | bytes 2064392 | tf_op jit(solution)/shard_map/ppermute | solution.py:38
  48.9 27.6 %collective-permute-start.4 = (bf16[96,3072]{1,0:T(8,128)(2,1)}, bf16[96,3072]{1,0:T(8,128)(2,1)}, u32[]{:S(2)}, u32[]{:S(2)}) collective-permute-start(bf16[96,3072]{1,0:T(8,128)(2,1)} %pad_maximum_fusion.17), channel_id=1, source_target_pairs={{0,16},{2,18},{4,20},{6,22},{8,24},{10,26},{12,28},{14,30},{16,0},... | collective-permute-start | bytes 1769480 | tf_op jit(solution)/shard_map/ppermute | solution.py:38
  63.7 29.7 %collective-permute-start.9 = (bf16[768,896]{1,0:T(8,128)(2,1)}, bf16[768,896]{1,0:T(8,128)(2,1)}, u32[]{:S(2)}, u32[]{:S(2)}) collective-permute-start(bf16[768,896]{1,0:T(8,128)(2,1)} %bitcast.18), channel_id=1, source_target_pairs={{0,4},{2,6},{4,0},{6,2},{8,12},{10,14},{12,8},{14,10},{16,20},{18,... | collective-permute-start | bytes 4128776 | tf_op jit(solution)/shard_map/ppermute | solution.py:38
  64.3 29.3 %collective-permute-start.8 = (bf16[768,896]{1,0:T(8,128)(2,1)S(1)}, bf16[768,896]{1,0:T(8,128)(2,1)}, u32[]{:S(2)}, u32[]{:S(2)}) collective-permute-start(bf16[768,896]{1,0:T(8,128)(2,1)S(1)} %bitcast.282), channel_id=1, source_target_pairs={{0,2},{2,0},{4,6},{6,4},{8,10},{10,8},{12,14},{14,12},{16,18},{18,... | collective-permute-start | bytes 4128776 | tf_op jit(solution)/shard_map/ppermute | solution.py:38
  77.9 27.1 %collective-permute-start.7 = (bf16[192,3072]{1,0:T(8,128)(2,1)S(1)}, bf16[192,3072]{1,0:T(8,128)(2,1)S(1)}, u32[]{:S(2)}, u32[]{:S(2)}) collective-permute-start(bf16[192,3072]{1,0:T(8,128)(2,1)S(1)} %bitcast.293), channel_id=1, source_target_pairs={{0,8},{2,10},{4,12},{6,14},{8,0},{10,2},{12,4},{14,6},{16,24},{18,... | collective-permute-start | bytes 3538952 | tf_op jit(solution)/shard_map/ppermute | solution.py:38
  107.5 29.6 %collective-permute-start.12 = (bf16[384,1536]{1,0:T(8,128)(2,1)}, bf16[384,1536]{1,0:T(8,128)(2,1)}, u32[]{:S(2)}, u32[]{:S(2)}) collective-permute-start(bf16[384,1536]{1,0:T(8,128)(2,1)} %get-tuple-element.457), channel_id=1, source_target_pairs={{0,4},{2,6},{4,0},{6,2},{8,12},{10,14},{12,8},{14,10},{16,20},{18,... | collective-permute-start | bytes 3538952 | tf_op jit(solution)/shard_map/ppermute | solution.py:38
  109.2 27.9 %collective-permute-start.13 = (bf16[384,1536]{1,0:T(8,128)(2,1)}, bf16[384,1536]{1,0:T(8,128)(2,1)}, u32[]{:S(2)}, u32[]{:S(2)}) collective-permute-start(bf16[384,1536]{1,0:T(8,128)(2,1)} %get-tuple-element.456), channel_id=1, source_target_pairs={{0,2},{2,0},{4,6},{6,4},{8,10},{10,8},{12,14},{14,12},{16,18},{18,... | collective-permute-start | bytes 3538952 | tf_op jit(solution)/shard_map/ppermute | solution.py:38
  123.2 38.1 %all-to-all-start = ((f32[16,8,1664]{2,1,0:T(8,128)}), f32[16,8,1664]{2,1,0:T(8,128)}, u32[]{:S(2)}, u32[]{:S(2)}) async-start(f32[16,8,1664]{2,1,0:T(8,128)} %pad_maximum_fusion.15), calls=%async_computation | async-start | bytes 1703936 | tf_op jit(solution)/shard_map/all_to_all | solution.py:195
  142.8 64.4 %collective-permute-start.15 = (bf16[768,1536]{1,0:T(8,128)(2,1)}, bf16[768,1536]{1,0:T(8,128)(2,1)}, u32[]{:S(2)}, u32[]{:S(2)}) collective-permute-start(bf16[768,1536]{1,0:T(8,128)(2,1)} %bitcast.56), channel_id=1, source_target_pairs={{0,4},{2,6},{4,0},{6,2},{8,12},{10,14},{12,8},{14,10},{16,20},{18,... | collective-permute-start | bytes 7077896 | tf_op jit(solution)/shard_map/ppermute | solution.py:38
  148.7 64.6 %collective-permute-start.14 = (bf16[768,1536]{1,0:T(8,128)(2,1)}, bf16[768,1536]{1,0:T(8,128)(2,1)}, u32[]{:S(2)}, u32[]{:S(2)}) collective-permute-start(bf16[768,1536]{1,0:T(8,128)(2,1)} %bitcast.51), channel_id=1, source_target_pairs={{0,2},{2,0},{4,6},{6,4},{8,10},{10,8},{12,14},{14,12},{16,18},{18,... | collective-permute-start | bytes 7077896 | tf_op jit(solution)/shard_map/ppermute | solution.py:38
  165.2 41.9 %all-to-all-start.1 = ((f32[16,8,1536]{2,1,0:T(8,128)}), f32[16,8,1536]{2,1,0:T(8,128)}, u32[]{:S(2)}, u32[]{:S(2)}) async-start(f32[16,8,1536]{2,1,0:T(8,128)} %walk.2), calls=%async_computation.1 | async-start | bytes 1572864 | tf_op jit(solution)/shard_map/all_to_all | solution.py:206
  237.3 40.6 %all-to-all-start.2 = ((f32[16,8,1536]{2,1,0:T(8,128)}), f32[16,8,1536]{2,1,0:T(8,128)}, u32[]{:S(2)}, u32[]{:S(2)}) async-start(f32[16,8,1536]{2,1,0:T(8,128)} %bitcast.332), calls=%async_computation.2 | async-start | bytes 1572864 | tf_op jit(solution)/shard_map/all_to_all | solution.py:195
  280.1 27.3 %all-to-all-start.3 = ((f32[16,8,1536]{2,1,0:T(8,128)}), f32[16,8,1536]{2,1,0:T(8,128)}, u32[]{:S(2)}, u32[]{:S(2)}) async-start(f32[16,8,1536]{2,1,0:T(8,128)} %walk.3), calls=%async_computation.3 | async-start | bytes 1572864 | tf_op jit(solution)/shard_map/all_to_all | solution.py:206
  288.4 43.4 %collective-permute-start.19 = (bf16[768,768]{1,0:T(8,128)(2,1)}, bf16[768,768]{1,0:T(8,128)(2,1)}, u32[]{:S(2)}, u32[]{:S(2)}) collective-permute-start(bf16[768,768]{1,0:T(8,128)(2,1)} %convolution_convert_fusion.4), channel_id=1, source_target_pairs={{0,2},{2,0},{4,6},{6,4},{8,10},{10,8},{12,14},{14,12},{16,18},{18,... | collective-permute-start | bytes 3538952 | tf_op jit(solution)/shard_map/ppermute | solution.py:38
  290.5 41.4 %collective-permute-start.18 = (bf16[768,768]{1,0:T(8,128)(2,1)}, bf16[768,768]{1,0:T(8,128)(2,1)}, u32[]{:S(2)}, u32[]{:S(2)}) collective-permute-start(bf16[768,768]{1,0:T(8,128)(2,1)} %convolution_convert_fusion.5), channel_id=1, source_target_pairs={{0,4},{2,6},{4,0},{6,2},{8,12},{10,14},{12,8},{14,10},{16,20},{18,... | collective-permute-start | bytes 3538952 | tf_op jit(solution)/shard_map/ppermute | solution.py:38
  297.9 51.0 %collective-permute-start.21 = (bf16[768,768]{1,0:T(8,128)(2,1)}, bf16[768,768]{1,0:T(8,128)(2,1)}, u32[]{:S(2)}, u32[]{:S(2)}) collective-permute-start(bf16[768,768]{1,0:T(8,128)(2,1)} %convolution_convert_fusion.2), channel_id=1, source_target_pairs={{0,2},{2,0},{4,6},{6,4},{8,10},{10,8},{12,14},{14,12},{16,18},{18,... | collective-permute-start | bytes 3538952 | tf_op jit(solution)/shard_map/ppermute | solution.py:38
  300.2 48.6 %collective-permute-start.20 = (bf16[768,768]{1,0:T(8,128)(2,1)}, bf16[768,768]{1,0:T(8,128)(2,1)}, u32[]{:S(2)}, u32[]{:S(2)}) collective-permute-start(bf16[768,768]{1,0:T(8,128)(2,1)} %convolution_convert_fusion.3), channel_id=1, source_target_pairs={{0,4},{2,6},{4,0},{6,2},{8,12},{10,14},{12,8},{14,10},{16,20},{18,... | collective-permute-start | bytes 3538952 | tf_op jit(solution)/shard_map/ppermute | solution.py:38
  330.4 42.6 %collective-permute-start.22 = (f32[3,1664]{1,0:T(4,128)}, f32[3,1664]{1,0:T(4,128)}, u32[]{:S(2)}, u32[]{:S(2)}) collective-permute-start(f32[3,1664]{1,0:T(4,128)} %pad_add_fusion.3), channel_id=1, source_target_pairs={{2,0},{4,2},{6,4},{8,6},{10,8},{12,10},{14,12},{16,14},{18,16},{20... | collective-permute-start | bytes 59912 | tf_op jit(solution)/shard_map/ppermute | solution.py:33
  360.5 30.5 %collective-permute-start.24 = (bf16[384,1536]{1,0:T(8,128)(2,1)}, bf16[384,1536]{1,0:T(8,128)(2,1)}, u32[]{:S(2)}, u32[]{:S(2)}) collective-permute-start(bf16[384,1536]{1,0:T(8,128)(2,1)} %bitcast.79), channel_id=1, source_target_pairs={{0,4},{2,6},{4,0},{6,2},{8,12},{10,14},{12,8},{14,10},{16,20},{18,... | collective-permute-start | bytes 3538952 | tf_op jit(solution)/shard_map/ppermute | solution.py:38
  362.2 29.2 %collective-permute-start.23 = (bf16[384,1536]{1,0:T(8,128)(2,1)}, bf16[384,1536]{1,0:T(8,128)(2,1)}, u32[]{:S(2)}, u32[]{:S(2)}) collective-permute-start(bf16[384,1536]{1,0:T(8,128)(2,1)} %bitcast.77), channel_id=1, source_target_pairs={{0,2},{2,0},{4,6},{6,4},{8,10},{10,8},{12,14},{14,12},{16,18},{18,... | collective-permute-start | bytes 3538952 | tf_op jit(solution)/shard_map/ppermute | solution.py:38
  368.5 20.4 %collective-permute-start.38 = (f32[7,1664]{1,0:T(8,128)S(1)}, f32[7,1664]{1,0:T(8,128)S(1)}, u32[]{:S(2)}, u32[]{:S(2)}) collective-permute-start(f32[7,1664]{1,0:T(8,128)S(1)} %concatenate.80), channel_id=1, source_target_pairs={{0,8},{2,10},{4,12},{6,14},{8,0},{10,2},{12,4},{14,6},{16,24},{18,... | collective-permute-start | bytes 139784 | tf_op jit(solution)/shard_map/ppermute | solution.py:38
  378.0 44.7 %collective-permute-start.27 = (bf16[768,896]{1,0:T(8,128)(2,1)S(1)}, bf16[768,896]{1,0:T(8,128)(2,1)S(1)}, u32[]{:S(2)}, u32[]{:S(2)}) collective-permute-start(bf16[768,896]{1,0:T(8,128)(2,1)S(1)} %convolution_convert_fusion), channel_id=1, source_target_pairs={{0,4},{2,6},{4,0},{6,2},{8,12},{10,14},{12,8},{14,10},{16,20},{18,... | collective-permute-start | bytes 4128776 | tf_op jit(solution)/shard_map/ppermute | solution.py:38
  379.5 43.2 %collective-permute-start.26 = (bf16[768,896]{1,0:T(8,128)(2,1)S(1)}, bf16[768,896]{1,0:T(8,128)(2,1)S(1)}, u32[]{:S(2)}, u32[]{:S(2)}) collective-permute-start(bf16[768,896]{1,0:T(8,128)(2,1)S(1)} %convolution_convert_fusion.1), channel_id=1, source_target_pairs={{0,2},{2,0},{4,6},{6,4},{8,10},{10,8},{12,14},{14,12},{16,18},{18,... | collective-permute-start | bytes 4128776 | tf_op jit(solution)/shard_map/ppermute | solution.py:38
  389.0 37.5 %collective-permute-start.39 = (f32[7,1664]{1,0:T(8,128)S(1)}, f32[7,1664]{1,0:T(8,128)S(1)}, u32[]{:S(2)}, u32[]{:S(2)}) collective-permute-start(f32[7,1664]{1,0:T(8,128)S(1)} %add.445), channel_id=1, source_target_pairs={{0,16},{2,18},{4,20},{6,22},{8,24},{10,26},{12,28},{14,30},{16,0},... | collective-permute-start | bytes 139784 | tf_op jit(solution)/shard_map/ppermute | solution.py:38
  396.6 24.2 %collective-permute-start.28 = (bf16[192,1536]{1,0:T(8,128)(2,1)S(1)}, bf16[192,1536]{1,0:T(8,128)(2,1)S(1)}, u32[]{:S(2)}, u32[]{:S(2)}) collective-permute-start(bf16[192,1536]{1,0:T(8,128)(2,1)S(1)} %bitcast.339), channel_id=1, source_target_pairs={{0,8},{2,10},{4,12},{6,14},{8,0},{10,2},{12,4},{14,6},{16,24},{18,... | collective-permute-start | bytes 1769480 | tf_op jit(solution)/shard_map/ppermute | solution.py:38
  426.6 49.2 %collective-permute-start.33 = (bf16[96,1536]{1,0:T(8,128)(2,1)}, bf16[96,1536]{1,0:T(8,128)(2,1)}, u32[]{:S(2)}, u32[]{:S(2)}) collective-permute-start(bf16[96,1536]{1,0:T(8,128)(2,1)} %fusion.25), channel_id=1, source_target_pairs={{0,16},{2,18},{4,20},{6,22},{8,24},{10,26},{12,28},{14,30},{16,0},... | collective-permute-start | bytes 884744 | tf_op jit(solution)/shard_map/ppermute | solution.py:38
  427.9 48.0 %collective-permute-start.32 = (bf16[96,1536]{1,0:T(8,128)(2,1)}, bf16[96,1536]{1,0:T(8,128)(2,1)}, u32[]{:S(2)}, u32[]{:S(2)}) collective-permute-start(bf16[96,1536]{1,0:T(8,128)(2,1)} %fusion.24), channel_id=1, source_target_pairs={{0,16},{2,18},{4,20},{6,22},{8,24},{10,26},{12,28},{14,30},{16,0},... | collective-permute-start | bytes 884744 | tf_op jit(solution)/shard_map/ppermute | solution.py:38
  455.0 18.2 %collective-permute-start.36 = (bf16[192,1792]{1,0:T(8,128)(2,1)}, bf16[192,1792]{1,0:T(8,128)(2,1)}, u32[]{:S(2)}, u32[]{:S(2)}) collective-permute-start(bf16[192,1792]{1,0:T(8,128)(2,1)} %bitcast.123), channel_id=1, source_target_pairs={{0,8},{2,10},{4,12},{6,14},{8,0},{10,2},{12,4},{14,6},{16,24},{18,... | collective-permute-start | bytes 2064392 | tf_op jit(solution)/shard_map/ppermute | solution.py:38
  458.8 37.7 %collective-permute-start.30 = (f32[512,768]{1,0:T(8,128)}, f32[512,768]{1,0:T(8,128)}, u32[]{:S(2)}, u32[]{:S(2)}) collective-permute-start(f32[512,768]{1,0:T(8,128)} %slice_select_fusion.1), channel_id=1, source_target_pairs={{0,1},{1,0},{2,3},{3,2},{4,5},{5,4},{6,7},{7,6},{8,9},{9,8},{10,11... | collective-permute-start | bytes 4718600 | tf_op jit(solution)/shard_map/ppermute | solution.py:38
  475.8 24.7 %collective-permute-start.37 = (bf16[96,1792]{1,0:T(8,128)(2,1)S(1)}, bf16[96,1792]{1,0:T(8,128)(2,1)S(1)}, u32[]{:S(2)}, u32[]{:S(2)}) collective-permute-start(bf16[96,1792]{1,0:T(8,128)(2,1)S(1)} %fusion.23), channel_id=1, source_target_pairs={{0,16},{2,18},{4,20},{6,22},{8,24},{10,26},{12,28},{14,30},{16,0},... | collective-permute-start | bytes 1032200 | tf_op jit(solution)/shard_map/ppermute | solution.py:38
  (122 other events, 1114.6 us)
